TPU v7x, 1024 devices: a whole 4x8x16 slice. The times are simulated.
1024 devices in a mesh: seq: 128 (over x, z, core), chan: 8 (over y).
Axes of the slice: x: 4, y: 8, z: 16, core: 2. Of those that a mesh axis runs over, the one named last changes fastest.
Arguments:
- grad_out: bfloat16 [16384, 4096], P('seq', 'chan'), may hold values from -30 to 30
- gate_query: bfloat16 [16384, 4096], P('seq', 'chan'), may hold values from -5 to 5
- key_input: bfloat16 [16384, 4096], P('seq', 'chan'), may hold values from -5 to 5
- value_input: bfloat16 [16384, 4096], P('seq', 'chan'), may hold values from -5 to 5
- decay_rate: float32 [16, 4096], P(None, 'chan'), as said below
- pole_angle: float32 [16, 4096], P(None, 'chan'), may hold values from 0.2 to 3
- residue: float32 [2, 16, 4096], P(None, None, 'chan'), may hold values from -3 to 3
- skip_gain: float32 [4096], P('chan'), may hold values from -4 to 4
Outputs:
- grad_key: bfloat16 [16384, 4096], P('seq', 'chan')
- grad_value: bfloat16 [16384, 4096], P('seq', 'chan')
- grad_residue: float32 [2, 16, 4096], P(None, None, 'chan')
Inputs may be any that keep to these rules, and one draw needn't show every extreme that they name: `decay_rate`: each rate lies between 0.5 / 16384 and 1 / 30.
All inputs are finite; a program needn't handle non-finite values.
Results may differ from a plain program's by a relative error of at most 0.0049.
Values sent between devices are 32-bit elements; how exact they have to be, the bound alone decides.
No kernel may reach another device: no remote copies, remote signals or barrier semaphores. Data moves between devices by JAX's collectives and lax.ppermute only.
A program may use at most 64 MiB of HBM per device.

v0:
```python
import math

import jax
import jax.numpy as jnp
from jax import lax
from jax.sharding import PartitionSpec as P


def prefix(value, axis, combine, identity):
    size, index = (lax.axis_size(axis), lax.axis_index(axis))
    everything = jax.tree.map(lambda part: lax.all_gather(part, axis), value)
    start = jax.tree.map(
        lambda part, zero: jnp.broadcast_to(jnp.asarray(zero, part.dtype), part.shape),
        value,
        identity,
    )

    def turn(k, before):
        at = size - 1 - k
        reached = at > index
        new = combine(before, jax.tree.map(lambda part: part[at], everything))
        return jax.tree.map(lambda a, b: jnp.where(reached, a, b), new, before)

    return lax.fori_loop(0, size, turn, start)


def complex_times(first_real, first_imaginary, second_real, second_imaginary):
    return (
        first_real * second_real - first_imaginary * second_imaginary,
        first_real * second_imaginary + first_imaginary * second_real,
    )


def join_carries(earlier, latter):
    earlier_state, earlier_powers = earlier
    latter_state, latter_powers = latter
    carried = complex_times(latter_powers[0], latter_powers[1], earlier_state[0], earlier_state[1])
    product_powers = complex_times(
        latter_powers[0], latter_powers[1], earlier_powers[0], earlier_powers[1]
    )
    return (
        jnp.stack([latter_state[0] + carried[0], latter_state[1] + carried[1]]),
        jnp.stack([product_powers[0], product_powers[1]]),
    )


def on_device(
    grad_out, gate_query, key_input, value_input, decay_rate, pole_angle, residue, skip_gain
):
    row_count, chan_width = grad_out.shape
    mode_count = decay_rate.shape[0]
    mode_step = min(2, mode_count)
    weighted = grad_out.astype(jnp.float32) * gate_query.astype(jnp.float32)
    key_values = key_input.astype(jnp.float32)
    value_values = value_input.astype(jnp.float32)
    stored = key_values * value_values
    norm_scale = jnp.sqrt(1.0 - jnp.exp(-2.0 * decay_rate))
    residue_real = residue[0] * norm_scale
    residue_imaginary = residue[1] * norm_scale
    position = jnp.arange(row_count, dtype=jnp.float32)
    upper_ones = (position[:, None] <= position[None, :]).astype(jnp.float32)

    def twiddles(first_mode):
        last_mode = first_mode + mode_step
        exponent = position[:, None, None] * decay_rate[first_mode:last_mode][None]
        phases = position[:, None, None] * pole_angle[first_mode:last_mode][None]
        return (exponent, jnp.cos(phases), jnp.sin(phases))

    own_parts = []
    for first_mode in range(0, mode_count, mode_step):
        exponent, cosine_turn, sine_turn = twiddles(first_mode)
        fading = jnp.exp(-exponent) * weighted[:, None, :]
        own_parts.append(
            jnp.stack([jnp.sum(fading * cosine_turn, axis=0), -jnp.sum(fading * sine_turn, axis=0)])
        )
    own_carry = jnp.concatenate(own_parts, axis=1)
    span_decay = jnp.exp(-row_count * decay_rate)
    span_turn = row_count * pole_angle
    span_powers = jnp.stack([span_decay * jnp.cos(span_turn), -span_decay * jnp.sin(span_turn)])
    identity = (
        jnp.zeros_like(own_carry),
        jnp.stack([jnp.ones_like(span_decay), jnp.zeros_like(span_decay)]),
    )
    incoming, _ = prefix((own_carry, span_powers), "seq", join_carries, identity)
    carried = complex_times(span_powers[0], span_powers[1], incoming[0], incoming[1])
    carried_real, carried_imaginary = carried
    signal_sum = skip_gain * weighted
    stored_rows = stored[:, None, :]
    residue_parts = []
    for first_mode in range(0, mode_count, mode_step):
        last_mode = first_mode + mode_step
        exponent, cosine_turn, sine_turn = twiddles(first_mode)
        fading = jnp.exp(-exponent) * weighted[:, None, :]
        source = jnp.stack([fading * cosine_turn, -fading * sine_turn], axis=1)
        summed = jnp.dot(
            upper_ones, source.reshape(row_count, -1), precision=lax.Precision.HIGHEST
        ).reshape(source.shape)
        whole_real = summed[:, 0] + carried_real[first_mode:last_mode][None]
        whole_imaginary = summed[:, 1] + carried_imaginary[first_mode:last_mode][None]
        growth = jnp.exp(exponent)
        back_real = growth * (cosine_turn * whole_real - sine_turn * whole_imaginary)
        back_imaginary = growth * (cosine_turn * whole_imaginary + sine_turn * whole_real)
        signal_sum = signal_sum + jnp.sum(
            residue_real[first_mode:last_mode] * back_real
            - residue_imaginary[first_mode:last_mode] * back_imaginary,
            axis=1,
        )
        residue_parts.append(
            jnp.stack(
                [
                    jnp.sum(stored_rows * back_real, axis=0),
                    jnp.sum(stored_rows * back_imaginary, axis=0),
                ]
            )
        )
    total_sums = jnp.concatenate(residue_parts, axis=1)
    grad_key = (signal_sum * value_values).astype(jnp.bfloat16)
    grad_value = (signal_sum * key_values).astype(jnp.bfloat16)
    raw_local = jnp.stack([norm_scale * total_sums[0], -norm_scale * total_sums[1]])
    clip_level = math.sqrt(2 * mode_count * chan_width * lax.axis_size("chan"))
    whole_sum = lax.psum(raw_local, "seq")
    squares = lax.psum(jnp.sum(whole_sum * whole_sum), "chan")
    grad_residue = whole_sum * (clip_level / jnp.maximum(jnp.sqrt(squares), clip_level))
    return (grad_key, grad_value, grad_residue)


def solution(mesh):
    return jax.shard_map(
        on_device,
        mesh=mesh,
        in_specs=(
            P("seq", "chan"),
            P("seq", "chan"),
            P("seq", "chan"),
            P("seq", "chan"),
            P(None, "chan"),
            P(None, "chan"),
            P(None, None, "chan"),
            P("chan"),
        ),
        out_specs=(P("seq", "chan"), P("seq", "chan"), P(None, None, "chan")),
        check_vma=False,
    )
```

profile of v0, /device:TPU:1, one launch (start us, length us, event | category | flops | bytes accessed | tf_op | source)
XLA Modules:
  0.0 818.5 jit_solution(18350742556271901911)
XLA Ops:
  8.8 0.9 fusion.98
  10.8 1.0 convert_multiply_fusion.3
  11.8 16.1 %multiply_reduce_fusion.17 = (f32[2,512]{1,0:T(2,128)S(1)}, f32[2,512]{1,0:T(2,128)S(1)}, f32[2,512]{1,0:T(2,128)S(1)}, f32[2,512]{1,0:T(2,128)S(1)}, f32[2,512]...) fusion(f32[2,512]{1,0:T(2,128)S(1)} %get-tuple-element.320, ...), kind=kLoop, calls=%fused_computation.141 | loop fusion | flops 8372224 | bytes 393216 | tf_op jit(solution)/shard_map/reduce_sum | solution.py:74
  28.1 1.3 concatenate.6
  29.7 16.1 %cosine_multiply_fusion.7 = (f32[128,1,2,512]{0,3,2,1:T(8,128)S(1)}, f32[128,1,2,512]{0,3,2,1:T(8,128)S(1)}, f32[128,1,2,512]{0,3,2,1:T(8,128)S(1)}, f32[128,1,2...) fusion(f32[2,512]{1,0:T(2,128)S(1)} %get-tuple-element.319, ...), kind=kLoop, calls=%fused_computation.200 | loop fusion | flops 7340032 | bytes 8716288 | tf_op jit(solution)/shard_map/mul | solution.py:94
  45.9 1.7 fusion.2
  47.7 1.7 fusion.5
  49.4 1.7 fusion.8
  52.4 1.7 fusion.17
  54.1 1.7 fusion.20
  56.5 119.5 %all-gather.7.cloned.1.call-done = f32[256,16,512]{2,1,0:T(8,128)} async-done(((f32[2,16,512]{2,1,0:T(8,128)}), f32[256,16,512]{2,1,0:T(8,128)}) %all-gather.7.cloned.1.call-update) | async-done | bytes 8388624 | tf_op jit(solution)/shard_map/all_gather | solution.py:11
  176.0 153.2 %all-gather.5.cloned.1.call-done = f32[256,16,512]{2,1,0:T(8,128)} async-done(((f32[2,16,512]{2,1,0:T(8,128)}), f32[256,16,512]{2,1,0:T(8,128)}) %all-gather.5.cloned.1.call-update) | async-done | bytes 8388624 | tf_op jit(solution)/shard_map/all_gather | solution.py:11
  329.1 116.6 %while.16 = (s32[]{:T(128)}, f32[2,16,512]{2,1,0:T(8,128)S(1)}, s32[]{:T(128)}, f32[128,2,16,512]{3,2,1,0:T(8,128)}, f32[128,2,16,512]{3,2,1,0:T(8,128)}, /*inde...) while((s32[]{:T(128)}, f32[2,16,512]{2,1,0:T(8,128)S(1)}, s32[]{:T(128)}, ...), condition=%wide.region_17.18_spmd.clone, body=%wide.region_16.17_spmd.clone.sunk | while | flops 131081 | bytes 590020 | solution.py:24
  445.7 0.9 bitcast_multiply_fusion.5
  446.8 7.8 multiply_reduce_fusion.15
  454.6 7.8 multiply_reduce_fusion.13
  462.4 6.6 multiply_reduce_fusion.9
  469.0 4.6 multiply_reduce_fusion.7
  474.5 2.4 fusion.67
  476.8 315.8 %all-reduce.2.cloned.1.call-done = f32[2,16,512]{2,1,0:T(8,128)} async-done(((f32[2,16,512]{2,1,0:T(8,128)}), f32[2,16,512]{2,1,0:T(8,128)}) %all-reduce.2.cloned.1.call-update) | async-done | bytes 65552 | tf_op jit(solution)/shard_map/psum | solution.py:121
  792.7 1.5 multiply_reduce_fusion.32
  794.1 1.6 fusion.66
  795.7 14.1 %psum.15 = f32[]{:T(128)} all-reduce(f32[]{:T(128)} %multiply_reduce_fusion.32), channel_id=1, replica_groups=mesh['seq'=128,'chan'=8] {'chan'}, use_global_device_ids=true, to_apply=%region_44.45 | all-reduce | flops 1 | bytes 8 | tf_op jit(solution)/shard_map/psum | solution.py:122
  810.5 1.5 broadcast_multiply_fusion
  (458 shorter events, 116.9 us)
Async XLA Ops:
  7.2 168.8 %all-gather.7.cloned.1.call-start = ((), (), s32[]{:S(2)}) async-start(), calls=%async_computation.2 | async-start | bytes 8454144 | tf_op jit(solution)/shard_map/all_gather | solution.py:11
  8.8 320.4 %all-gather.5.cloned.1.call-start = ((), (), s32[]{:S(2)}) async-start(), calls=%async_computation.1 | async-start | bytes 8454144 | tf_op jit(solution)/shard_map/all_gather | solution.py:11
  9.8 37.8 %copy-start.4 = (f32[2,512]{1,0:T(2,128)}, f32[2,512]{1,0:T(2,128)S(1)}, u32[]{:S(2)}) copy-start(f32[2,512]{1,0:T(2,128)S(1)} %get-tuple-element.317) | copy-start | bytes 12292
  9.8 37.8 %copy-start.5 = (f32[2,512]{1,0:T(2,128)}, f32[2,512]{1,0:T(2,128)S(1)}, u32[]{:S(2)}) copy-start(f32[2,512]{1,0:T(2,128)S(1)} %get-tuple-element.321) | copy-start | bytes 12292
  9.8 37.8 %copy-start.8 = (f32[2,512]{1,0:T(2,128)}, f32[2,512]{1,0:T(2,128)S(1)}, u32[]{:S(2)}) copy-start(f32[2,512]{1,0:T(2,128)S(1)} %get-tuple-element.314) | copy-start | bytes 12292
  9.8 37.8 %copy-start.9 = (f32[2,512]{1,0:T(2,128)}, f32[2,512]{1,0:T(2,128)S(1)}, u32[]{:S(2)}) copy-start(f32[2,512]{1,0:T(2,128)S(1)} %get-tuple-element.315) | copy-start | bytes 12292
  9.8 37.8 %copy-start.12 = (f32[2,512]{1,0:T(2,128)}, f32[2,512]{1,0:T(2,128)S(1)}, u32[]{:S(2)}) copy-start(f32[2,512]{1,0:T(2,128)S(1)} %get-tuple-element.318) | copy-start | bytes 12292
  9.8 37.8 %copy-start.13 = (f32[2,512]{1,0:T(2,128)}, f32[2,512]{1,0:T(2,128)S(1)}, u32[]{:S(2)}) copy-start(f32[2,512]{1,0:T(2,128)S(1)} %get-tuple-element.319) | copy-start | bytes 12292
  10.8 36.9 %copy-start.6 = (f32[2,512]{1,0:T(2,128)}, f32[2,512]{1,0:T(2,128)S(1)}, u32[]{:S(2)}) copy-start(f32[2,512]{1,0:T(2,128)S(1)} %get-tuple-element.309) | copy-start | bytes 12292
  10.8 36.9 %copy-start.7 = (f32[2,512]{1,0:T(2,128)}, f32[2,512]{1,0:T(2,128)S(1)}, u32[]{:S(2)}) copy-start(f32[2,512]{1,0:T(2,128)S(1)} %get-tuple-element.313) | copy-start | bytes 12292
  10.8 36.9 %copy-start.10 = (f32[2,512]{1,0:T(2,128)}, f32[2,512]{1,0:T(2,128)S(1)}, u32[]{:S(2)}) copy-start(f32[2,512]{1,0:T(2,128)S(1)} %get-tuple-element.306) | copy-start | bytes 12292
  10.8 36.9 %copy-start.11 = (f32[2,512]{1,0:T(2,128)}, f32[2,512]{1,0:T(2,128)S(1)}, u32[]{:S(2)}) copy-start(f32[2,512]{1,0:T(2,128)S(1)} %get-tuple-element.307) | copy-start | bytes 12292
  10.8 36.9 %copy-start.14 = (f32[2,512]{1,0:T(2,128)}, f32[2,512]{1,0:T(2,128)S(1)}, u32[]{:S(2)}) copy-start(f32[2,512]{1,0:T(2,128)S(1)} %get-tuple-element.310) | copy-start | bytes 12292
  10.8 36.9 %copy-start.15 = (f32[2,512]{1,0:T(2,128)}, f32[2,512]{1,0:T(2,128)S(1)}, u32[]{:S(2)}) copy-start(f32[2,512]{1,0:T(2,128)S(1)} %get-tuple-element.311) | copy-start | bytes 12292
  29.4 763.3 %all-reduce.2.cloned.1.call-start = ((), (), s32[]{:S(2)}) async-start(), calls=%async_computation | async-start | bytes 131072 | tf_op jit(solution)/shard_map/psum | solution.py:121
  45.9 10.6 %copy-start.1 = (bf16[128,512]{1,0:T(8,128)(2,1)S(1)}, bf16[128,512]{1,0:T(8,128)(2,1)}, u32[]{:S(2)}) copy-start(bf16[128,512]{1,0:T(8,128)(2,1)} %param.12) | copy-start | bytes 393220
  45.9 10.6 %copy-start.2 = (bf16[128,512]{1,0:T(8,128)(2,1)S(1)}, bf16[128,512]{1,0:T(8,128)(2,1)}, u32[]{:S(2)}) copy-start(bf16[128,512]{1,0:T(8,128)(2,1)} %param.13) | copy-start | bytes 393220
  49.4 396.4 %copy-start = (f32[16,512]{1,0:T(8,128)S(1)}, f32[16,512]{1,0:T(8,128)}, u32[]{:S(2)}) copy-start(f32[16,512]{1,0:T(8,128)} %param.14) | copy-start | bytes 98308
  49.4 396.4 %copy-start.3 = (f32[16,512]{1,0:T(8,128)S(1)}, f32[16,512]{1,0:T(8,128)}, u32[]{:S(2)}) copy-start(f32[16,512]{1,0:T(8,128)} %param.15) | copy-start | bytes 98308
Sparse Core Ops, SparseCore 0:
  12.9 163.0 all-gather.6
  180.9 148.2 all-gather.4
  474.6 318.0 all-reduce.1
where the time goes:
time: 832 us; the launch traced here: 818 us
  waiting for transfers between devices  589 us (71%)
  other arithmetic  181 us (22%)
  between operations  14.9 us (2%)
  blocking collectives  14.1 us (2%)
  matrix products  10.4 us (1%)
    psum x1, waiting for transfers between devices, on_device(): whole_sum = lax.psum(raw_local, 'seq')  316 us
    all_gather x2, waiting for transfers between devices, prefix(): everything = jax.tree.map(lambda part: lax.all_gather(part, axis), value)  273 us
    add x128, other arithmetic, join_carries(): latter_state[0] + carried[0]  107 us
    reduce_sum x4, other arithmetic, on_device(): jnp.sum(stored_rows * back_real, axis=0)  26.8 us
  transfers between devices with their start and end apart: 3, of which 3 were waited for; matrix products, arithmetic and copies ran while one was open for 6% of the time, Pallas kernels for 0%

commit v1 on v0

v1 whole, which is shorter than its diff:
```python
import functools
import math

import jax
import jax.numpy as jnp
from jax import lax
from jax.experimental import pallas as pl
from jax.experimental.pallas import tpu as pltpu
from jax.sharding import PartitionSpec as P

LANES = 128
HALF = 64
SUB = 8
TURN_PARTS = (1.5703125, 4.837512969970703e-4, 7.54978995489188e-8)


def sine_cosine(angle):
    quarter = jnp.floor(angle * (2.0 / math.pi) + 0.5)
    rest = angle
    for part in TURN_PARTS:
        rest = rest - quarter * part
    square = rest * rest
    sine = ((-1.9515295891e-4 * square + 8.3321608736e-3) * square - 1.6666654611e-1) * square * rest + rest
    cosine = ((2.443315711809948e-5 * square - 1.388731625493765e-3) * square + 4.166664568298827e-2) * square * square
    cosine = cosine - 0.5 * square + 1.0
    index = quarter - 4.0 * jnp.floor(quarter * 0.25)
    odd = (index == 1.0) | (index == 3.0)
    sine_out = jnp.where(odd, cosine, sine)
    cosine_out = jnp.where(odd, sine, cosine)
    sine_out = jnp.where(index >= 2.0, -sine_out, sine_out)
    cosine_out = jnp.where((index == 1.0) | (index == 2.0), -cosine_out, cosine_out)
    return sine_out, cosine_out


def scale_of(decay):
    twice = 2.0 * decay
    series = 1.0 - twice * (1.0 / 7.0)
    for divisor in (6.0, 5.0, 4.0, 3.0, 2.0):
        series = 1.0 - twice * (1.0 / divisor) * series
    return jnp.sqrt(jnp.where(twice < 0.25, twice * series, 1.0 - jnp.exp(-twice)))


def spread(ref, row, columns=slice(None)):
    return jnp.broadcast_to(ref[pl.ds(row, 1), columns], (SUB, ref[pl.ds(row, 1), columns].shape[1]))


def lane_low(shape):
    return lax.broadcasted_iota(jnp.int32, shape, 1) < HALF


def pack_slices(real, imaginary, store):
    modes, width = real.shape
    low = lane_low((modes, LANES))
    for tile in range(width // LANES):
        re = real[:, tile * LANES : (tile + 1) * LANES]
        im = imaginary[:, tile * LANES : (tile + 1) * LANES]
        store(2 * tile * modes, jnp.where(low, re, pltpu.roll(im, HALF, 1)))
        store((2 * tile + 1) * modes, jnp.where(low, pltpu.roll(re, HALF, 1), im))


def unpack_slices(load, modes, width):
    low = lane_low((modes, LANES))
    reals, imaginaries = [], []
    for tile in range(width // LANES):
        even, odd = load(2 * tile * modes), load((2 * tile + 1) * modes)
        reals.append(jnp.where(low, even, pltpu.roll(odd, HALF, 1)))
        imaginaries.append(jnp.where(low, pltpu.roll(even, HALF, 1), odd))
    return jnp.concatenate(reals, axis=1), jnp.concatenate(imaginaries, axis=1)


def local_kernel(grad_ref, gate_ref, key_ref, value_ref, decay_ref, angle_ref, packed_ref, power_ref, weighted, stored):
    rows = grad_ref.shape[0]
    modes, width = decay_ref.shape
    weighted[...] = grad_ref[...].astype(jnp.float32) * gate_ref[...].astype(jnp.float32)
    stored[...] = key_ref[...].astype(jnp.float32) * value_ref[...].astype(jnp.float32)
    decay, angle = decay_ref[...], angle_ref[...]
    sine, cosine = sine_cosine(angle)
    radius = jnp.exp(-decay)
    step_real, step_imaginary = radius * cosine, -radius * sine
    span_sine, span_cosine = sine_cosine(angle * float(rows))
    span_radius = jnp.exp(-decay * float(rows))
    power_real, power_imaginary = span_radius * span_cosine, -span_radius * span_sine

    def store_power(column):
        def store(row, value):
            power_ref[row : row + modes, column : column + LANES] = value

        return store

    pack_slices(power_real, power_real, store_power(0))
    pack_slices(-power_imaginary, power_imaginary, store_power(LANES))
    parts = [[] for _ in range(6)]
    for first in range(0, modes, SUB):
        sr, si = step_real[first : first + SUB], step_imaginary[first : first + SUB]

        def block(j, carry, sr=sr, si=si):
            br, bi, lr, li, kr, ki = carry
            for r in range(SUB):
                t = rows - 1 - (j * SUB + r)
                w, s, s_up = spread(weighted, t), spread(stored, t), spread(stored, j * SUB + r)
                br, bi = (w + sr * br) - si * bi, sr * bi + si * br
                lr, li = lr + s * br, li + s * bi
                kr = kr + s_up
                kr, ki = sr * kr - si * ki, sr * ki + si * kr
            return br, bi, lr, li, kr, ki

        zero = jnp.zeros((SUB, width), jnp.float32)
        done = lax.fori_loop(0, rows // SUB, block, (zero,) * 6)
        for part, value in zip(parts, done):
            part.append(value)
    whole = [jnp.concatenate(part, axis=0) for part in parts]
    for which in range(3):

        def store(row, value, column=which * LANES):
            packed_ref[row : row + modes, column : column + LANES] = value

        pack_slices(whole[2 * which], whole[2 * which + 1], store)


def times(first, second_direct, second_cross):
    return first * second_direct + pltpu.roll(first, HALF, 1) * second_cross


def scan_kernel(where_ref, packed_ref, power_ref, out_ref):
    rows = packed_ref.shape[0]
    low = lane_low((1, LANES))
    mine = lax.broadcasted_iota(jnp.int32, power_ref.shape, 0) == where_ref[0]
    power = jnp.sum(jnp.where(mine, power_ref[...], 0.0), axis=0, keepdims=True)
    direct, cross = power[:, 0:LANES], power[:, LANES : 2 * LANES]
    state = packed_ref[:, 0:LANES]
    index = lax.broadcasted_iota(jnp.int32, (rows, LANES), 0)

    def from_later(value, shift):
        return jnp.where(index < rows - shift, pltpu.roll(value, rows - shift, 0), 0.0)

    state = from_later(state, 1)
    shift = 1
    while shift < rows:
        state = state + times(from_later(state, shift), direct, cross)
        real = jnp.where(low, direct, pltpu.roll(direct, HALF, 1))
        direct, cross = real * real - cross * cross, 2.0 * real * cross
        shift *= 2
    sums = packed_ref[:, LANES : 2 * LANES]
    reach = packed_ref[:, 2 * LANES : 3 * LANES]
    swapped = pltpu.roll(reach, HALF, 1)
    low_rows = lane_low((rows, LANES))
    reach_direct = jnp.where(low_rows, reach, swapped)
    reach_cross = jnp.where(low_rows, -swapped, reach)
    total = jnp.sum(sums + times(state, reach_direct, reach_cross), axis=0, keepdims=True)
    out_ref[:, 0:LANES] = state
    out_ref[:, LANES : 2 * LANES] = jnp.broadcast_to(total, (rows, LANES))


def residue_kernel(back_ref, decay_ref, raw_ref, squares_ref):
    modes, width = decay_ref.shape
    scale = scale_of(decay_ref[...])
    real, imaginary = unpack_slices(lambda row: back_ref[row : row + modes, LANES : 2 * LANES], modes, width)
    real, imaginary = real * scale, -(imaginary * scale)
    raw_ref[0] = real
    raw_ref[1] = imaginary
    squares = jnp.sum(real * real + imaginary * imaginary, axis=0, keepdims=True)
    total = squares[:, 0:LANES]
    for tile in range(1, width // LANES):
        total = total + squares[:, tile * LANES : (tile + 1) * LANES]
    squares_ref[...] = jnp.broadcast_to(total, squares_ref.shape)


def signal_kernel(
    back_ref, grad_ref, gate_ref, key_ref, value_ref, decay_ref, angle_ref, residue_ref, skip_ref,
    grad_key_ref, grad_value_ref, weighted, signal,
):
    rows = grad_ref.shape[0]
    modes, width = decay_ref.shape
    weighted[...] = grad_ref[...].astype(jnp.float32) * gate_ref[...].astype(jnp.float32)
    decay = decay_ref[...]
    sine, cosine = sine_cosine(angle_ref[...])
    radius = jnp.exp(-decay)
    step_real, step_imaginary = radius * cosine, -radius * sine
    scale = scale_of(decay)
    weight_real, weight_imaginary = residue_ref[0] * scale, residue_ref[1] * scale
    real, imaginary = unpack_slices(lambda row: back_ref[row : row + modes, 0:LANES], modes, width)
    start_real = weight_real * real - weight_imaginary * imaginary
    start_imaginary = weight_real * imaginary + weight_imaginary * real
    span = 2 * LANES
    for column in range(0, width, span):
        cut = slice(column, column + span)
        steps = [
            tuple(a[first : first + SUB, cut] for a in (step_real, step_imaginary, weight_real, weight_imaginary))
            for first in range(0, modes, SUB)
        ]
        begin = tuple(
            a[first : first + SUB, cut] for first in range(0, modes, SUB) for a in (start_real, start_imaginary)
        )

        def block(j, carry, steps=steps, cut=cut):
            carry = list(carry)
            for r in range(SUB):
                t = rows - 1 - (j * SUB + r)
                w = spread(weighted, t, cut)
                total = None
                for which, (sr, si, cr, ci) in enumerate(steps):
                    qr, qi = carry[2 * which], carry[2 * which + 1]
                    qr, qi = (cr * w + sr * qr) - si * qi, (ci * w + sr * qi) + si * qr
                    carry[2 * which], carry[2 * which + 1] = qr, qi
                    total = qr if total is None else total + qr
                place = pl.ds(pl.multiple_of(t * SUB, SUB), SUB)
                for part in range(span // LANES):
                    view = signal.at[cut.start // LANES + part]
                    view[place, :] = total[:, part * LANES : (part + 1) * LANES]
            return tuple(carry)

        lax.fori_loop(0, rows // SUB, block, begin)
    summed = skip_ref[...] * weighted[...]
    for tile in range(width // LANES):
        cut = slice(tile * LANES, (tile + 1) * LANES)
        part = summed[:, cut]
        view = signal.at[tile]
        for member in range(SUB):
            part = part + view[pl.ds(member, rows, stride=SUB), :]
        grad_key_ref[:, cut] = (part * value_ref[:, cut].astype(jnp.float32)).astype(jnp.bfloat16)
        grad_value_ref[:, cut] = (part * key_ref[:, cut].astype(jnp.float32)).astype(jnp.bfloat16)


def clip_kernel(clip_level, squares_ref, raw_ref, out_ref):
    norm = jnp.sqrt(jnp.sum(squares_ref[...], keepdims=True))
    out_ref[...] = raw_ref[...] * (clip_level / jnp.maximum(norm, clip_level))[None]


def on_device(
    grad_out, gate_query, key_input, value_input, decay_rate, pole_angle, residue, skip_gain
):
    rows, width = grad_out.shape
    modes = decay_rate.shape[0]
    shards, chan_shards = lax.axis_size("seq"), lax.axis_size("chan")
    slices = modes * width // HALF
    packed, power = pl.pallas_call(
        local_kernel,
        out_shape=(
            jax.ShapeDtypeStruct((slices, 3 * LANES), jnp.float32),
            jax.ShapeDtypeStruct((slices, 2 * LANES), jnp.float32),
        ),
        scratch_shapes=[pltpu.VMEM((rows, width), jnp.float32)] * 2,
        name="local_pass",
    )(grad_out, gate_query, key_input, value_input, decay_rate, pole_angle)
    turned = lax.all_to_all(packed, "seq", 0, 0, tiled=True)
    where = lax.axis_index("seq").reshape(1)
    answers = pl.pallas_call(
        scan_kernel,
        in_specs=[pl.BlockSpec(memory_space=pltpu.SMEM)] + [pl.BlockSpec(memory_space=pltpu.VMEM)] * 2,
        out_shape=jax.ShapeDtypeStruct((shards, 2 * LANES), jnp.float32),
        name="scan_shards",
    )(where, turned, power)
    back = lax.all_to_all(answers, "seq", 0, 0, tiled=True)
    raw, squares = pl.pallas_call(
        residue_kernel,
        out_shape=(
            jax.ShapeDtypeStruct((2, modes, width), jnp.float32),
            jax.ShapeDtypeStruct((chan_shards, LANES), jnp.float32),
        ),
        name="residue_sums",
    )(back, decay_rate)
    all_squares = lax.all_to_all(squares, "chan", 0, 0, tiled=True)
    grad_key, grad_value = pl.pallas_call(
        signal_kernel,
        out_shape=(jax.ShapeDtypeStruct((rows, width), jnp.bfloat16),) * 2,
        scratch_shapes=[
            pltpu.VMEM((rows, width), jnp.float32),
            pltpu.VMEM((width // LANES, rows * SUB, LANES), jnp.float32),
        ],
        cost_estimate=pl.CostEstimate(flops=20 * rows * width * modes, bytes_accessed=12 * rows * width, transcendentals=0),
        name="signal_pass",
    )(back, grad_out, gate_query, key_input, value_input, decay_rate, pole_angle, residue, skip_gain.reshape(1, width))
    clip_level = math.sqrt(2 * modes * width * chan_shards)
    grad_residue = pl.pallas_call(
        functools.partial(clip_kernel, clip_level),
        out_shape=jax.ShapeDtypeStruct((2, modes, width), jnp.float32),
        name="clip",
    )(all_squares, raw)
    return (grad_key, grad_value, grad_residue)


def solution(mesh):
    return jax.shard_map(
        on_device,
        mesh=mesh,
        in_specs=(
            P("seq", "chan"),
            P("seq", "chan"),
            P("seq", "chan"),
            P("seq", "chan"),
            P(None, "chan"),
            P(None, "chan"),
            P(None, None, "chan"),
            P("chan"),
        ),
        out_specs=(P("seq", "chan"), P("seq", "chan"), P(None, None, "chan")),
        check_vma=False,
    )
```

time: 832 us -> 98.1 us (0.12); the launches traced: 818 us -> 96.9 us
  waiting for transfers between devices: 589 us -> 22.4 us
  other arithmetic: 181 us -> 0 us
  starting transfers between devices: 0.3 us -> 30.9 us
  Pallas kernels: 0 us -> 14.3 us
  between operations: 14.9 us -> 0.65 us
  matrix products: 10.4 us -> 0 us
  blocking collectives: 14.1 us -> 23.9 us
    psum x1 -> x0, waiting for transfers between devices: 316 us -> none  [on_device(): whole_sum = lax.psum(raw_local, 'seq')]
    all_gather x2 -> x0, waiting for transfers between devices: 273 us -> none  [prefix(): everything = jax.tree.map(lambda part: lax.all_gather(part, axis), value)]
    add x128 -> x0, other arithmetic: 107 us -> none  [join_carries(): latter_state[0] + carried[0]]
    reduce_sum x6 -> x0, other arithmetic: 44.4 us -> none  [the longest x4 26.8 us: on_device(): jnp.sum(stored_rows * back_real, axis=0)]
    all_to_all x0 -> x2, starting transfers between devices: none -> 30.9 us  [the longest x1 24.1 us: on_device(): turned = lax.all_to_all(packed, 'seq', 0, 0, tiled=True)]
    all_to_all x0 -> x1, blocking collectives: none -> 23.9 us  [on_device(): back = lax.all_to_all(answers, 'seq', 0, 0, tiled=True)]
    all_to_all x0 -> x2, waiting for transfers between devices: none -> 22.4 us  [the longest x1 20 us: on_device(): turned = lax.all_to_all(packed, 'seq', 0, 0, tiled=True)]
    mul x5 -> x0, other arithmetic: 19.6 us -> none  [the longest x1 16.1 us: on_device(): source = jnp.stack([fading * cosine_turn, -fading * sine_turn], axis=1)]
  transfers between devices with their start and end apart: 3 -> 2, of which waited for: 3 -> 2; matrix products, arithmetic and copies ran while one was open for 6% -> 0% of each run, Pallas kernels for 0% -> 4%
where the time goes in v1:
time: 98.1 us; the launch traced here: 96.9 us
  starting transfers between devices  30.9 us (31%)
  blocking collectives  23.9 us (24%)
  waiting for transfers between devices  22.4 us (23%)
  Pallas kernels  14.3 us (15%)
  local copies, waits for them, and re-layouts  4.77 us (5%)
    all_to_all x1, starting transfers between devices, on_device(): turned = lax.all_to_all(packed, 'seq', 0, 0, tiled=True)  24.1 us
    all_to_all x1, blocking collectives, on_device(): back = lax.all_to_all(answers, 'seq', 0, 0, tiled=True)  23.9 us
    all_to_all x1, waiting for transfers between devices, on_device(): turned = lax.all_to_all(packed, 'seq', 0, 0, tiled=True)  20 us
    all_to_all x1, starting transfers between devices, on_device(): all_squares = lax.all_to_all(squares, 'chan', 0, 0, tiled=True)  6.82 us
    pallas_call x1, Pallas kernels, on_device(): pl.pallas_call(local_kernel, out_shape=(jax.ShapeDtypeStruct((slices, 3 *...  4.83 us
    pallas_call x1, Pallas kernels, on_device(): pl.pallas_call(signal_kernel, out_shape=(jax.ShapeDtypeStruct((rows, widt...  3.97 us
    all_to_all x1, waiting for transfers between devices, on_device(): all_squares = lax.all_to_all(squares, 'chan', 0, 0, tiled=True)  2.49 us
    pallas_call x1, Pallas kernels, on_device(): pl.pallas_call(scan_kernel, in_specs=[pl.BlockSpec(memory_space=pltpu.SME...  2.29 us
  transfers between devices with their start and end apart: 2, of which 2 were waited for; matrix products, arithmetic and copies ran while one was open for 0% of the time, Pallas kernels for 4%

profile of v1, /device:TPU:1, one launch (start us, length us, event | category | flops | bytes accessed | tf_op | source)
XLA Modules:
  0.0 96.9 jit_solution(6676473457881503537)
XLA Ops:
  0.6 4.8 %local_pass.1 = (f32[128,384]{1,0:T(8,128)}, f32[128,256]{1,0:T(8,128)}) custom-call(bf16[128,512]{1,0:T(8,128)(2,1)} %grad_ref.3, bf16[128,512]{1,0:T(8,128)(2,1)} %gate_ref.3, bf16[128,512]{1,0:T(8,128)(2,1)} %key_ref.3, bf16[128,512]{1,0:T(8,128)(2,1)} %value_ref.3, f32[16,512]{1,0:T(8,128)} %decay_ref.5, f32[16,512]{1,0:T(8,128)} %angle_ref.3), custom_call_target="tpu_custom_call" | custom-call | tf_op jit(solution)/shard_map/local_pass/pallas_call | solution.py:236
  5.5 1.8 %copy.11 = f32[128,1,384]{2,1,0:T(1,128)} copy(f32[128,1,384]{2,0,1:T(8,128)} %bitcast.18) | data formatting | bytes 393216 | tf_op jit(solution)/shard_map/all_to_all | solution.py:245
  7.3 24.1 %all-to-all-start = ((f32[128,1,384]{2,1,0:T(1,128)}), f32[128,1,384]{2,1,0:T(1,128)S(1)}, u32[]{:S(2)}, u32[]{:S(2)}) async-start(f32[128,1,384]{2,1,0:T(1,128)} %copy.11), calls=%async_computation | async-start | bytes 393216 | tf_op jit(solution)/shard_map/all_to_all | solution.py:245
  31.3 20.0 %all-to-all-done = f32[128,1,384]{2,1,0:T(1,128)S(1)} async-done(((f32[128,1,384]{2,1,0:T(1,128)}), f32[128,1,384]{2,1,0:T(1,128)S(1)}, u32[]{:S(2)}, u32[]{:S(2)}) %all-to-all-start) | async-done | bytes 196640 | tf_op jit(solution)/shard_map/all_to_all | solution.py:245
  51.3 0.7 copy.18
  52.0 2.3 %scan_shards.1 = f32[128,256]{1,0:T(8,128)} custom-call(s32[1]{0:T(128)} %bitcast.where_ref, f32[128,384]{1,0:T(8,128)} %bitcast.16, f32[128,256]{1,0:T(8,128)} %get-tuple-element.10.power_ref), custom_call_target="tpu_custom_call" | custom-call | tf_op jit(solution)/shard_map/scan_shards/pallas_call | solution.py:247
  54.3 1.0 %copy.12 = f32[128,1,256]{2,1,0:T(1,128)S(1)} copy(f32[128,1,256]{2,0,1:T(8,128)} %bitcast.17) | data formatting | bytes 262144 | tf_op jit(solution)/shard_map/all_to_all | solution.py:253
  55.3 23.9 %all_to_all.33 = f32[128,1,256]{2,1,0:T(1,128)S(1)} all-to-all(f32[128,1,256]{2,1,0:T(1,128)S(1)} %copy.12), channel_id=1, replica_groups=mesh['seq'=128,'chan'=8] {'seq'}, dimensions={0} | all-to-all | bytes 262144 | tf_op jit(solution)/shard_map/all_to_all | solution.py:253
  79.2 0.7 copy.19
  79.8 1.6 %residue_sums.1 = (f32[2,16,512]{2,1,0:T(8,128)}, f32[8,128]{1,0:T(8,128)}) custom-call(f32[128,256]{1,0:T(8,128)} %bitcast.14, f32[16,512]{1,0:T(8,128)} %decay_ref.5), custom_call_target="tpu_custom_call" | custom-call | tf_op jit(solution)/shard_map/residue_sums/pallas_call | solution.py:254
  81.4 6.8 %all-to-all-start.2 = ((f32[8,1,128]{2,1,0:T(1,128)}), f32[8,1,128]{2,1,0:T(1,128)S(1)}, u32[]{:S(2)}, u32[]{:S(2)}) async-start(f32[8,1,128]{2,1,0:T(1,128)} %bitcast.20), calls=%async_computation.2 | async-start | bytes 8192 | tf_op jit(solution)/shard_map/all_to_all | solution.py:262
  88.3 4.0 %signal_pass.1 = (bf16[128,512]{1,0:T(8,128)(2,1)}, bf16[128,512]{1,0:T(8,128)(2,1)}) custom-call(f32[128,256]{1,0:T(8,128)} %bitcast.15, bf16[128,512]{1,0:T(8,128)(2,1)} %grad_ref.3, bf16[128,512]{1,0:T(8,128)(2,1)} %gate_ref.3, bf16[128,512]{1,0:T(8,128)(2,1)} %key_ref.3, bf16[128,512]{1,0:T(8,128)(2,1)} %value_ref.3, f32[16,512]{1,0:T(8,128)} %decay_ref.5, ...), custom_call_target="tpu_custom_call" | custom-call | flops 20971520 | bytes 786432 | tf_op jit(solution)/shard_map/signal_pass/pallas_call | solution.py:263
  92.2 2.5 %all-to-all-done.2 = f32[8,1,128]{2,1,0:T(1,128)S(1)} async-done(((f32[8,1,128]{2,1,0:T(1,128)}), f32[8,1,128]{2,1,0:T(1,128)S(1)}, u32[]{:S(2)}, u32[]{:S(2)}) %all-to-all-start.2) | async-done | bytes 4128 | tf_op jit(solution)/shard_map/all_to_all | solution.py:262
  94.7 0.0 copy-start
  94.7 0.6 copy-done
  95.3 1.6 %clip.1 = f32[2,16,512]{2,1,0:T(8,128)} custom-call(f32[8,128]{1,0:T(8,128)} %bitcast.19, f32[2,16,512]{2,1,0:T(8,128)} %get-tuple-element.14.raw_ref), custom_call_target="tpu_custom_call" | custom-call | tf_op jit(solution)/shard_map/clip/pallas_call | solution.py:274
Async XLA Ops:
  7.3 44.0 %all-to-all-start = ((f32[128,1,384]{2,1,0:T(1,128)}), f32[128,1,384]{2,1,0:T(1,128)S(1)}, u32[]{:S(2)}, u32[]{:S(2)}) async-start(f32[128,1,384]{2,1,0:T(1,128)} %copy.11), calls=%async_computation | async-start | bytes 393216 | tf_op jit(solution)/shard_map/all_to_all | solution.py:245
  81.4 13.3 %all-to-all-start.2 = ((f32[8,1,128]{2,1,0:T(1,128)}), f32[8,1,128]{2,1,0:T(1,128)S(1)}, u32[]{:S(2)}, u32[]{:S(2)}) async-start(f32[8,1,128]{2,1,0:T(1,128)} %bitcast.20), calls=%async_computation.2 | async-start | bytes 8192 | tf_op jit(solution)/shard_map/all_to_all | solution.py:262
  94.7 0.6 copy-start

commit v2 on v1

--- a/solution.py
+++ b/solution.py
@@ -40,8 +40,9 @@
     return jnp.sqrt(jnp.where(twice < 0.25, twice * series, 1.0 - jnp.exp(-twice)))
 
 
-def spread(ref, row, columns=slice(None)):
-    return jnp.broadcast_to(ref[pl.ds(row, 1), columns], (SUB, ref[pl.ds(row, 1), columns].shape[1]))
+def line_block(ref, first, columns=slice(None)):
+    block = ref[pl.ds(pl.multiple_of(first, SUB), SUB), columns]
+    return [jnp.broadcast_to(block[r : r + 1], block.shape) for r in range(SUB)]
 
 
 def lane_low(shape):
@@ -68,7 +69,7 @@
     return jnp.concatenate(reals, axis=1), jnp.concatenate(imaginaries, axis=1)
 
 
-def local_kernel(grad_ref, gate_ref, key_ref, value_ref, decay_ref, angle_ref, packed_ref, power_ref, weighted, stored):
+def local_kernel(grad_ref, gate_ref, key_ref, value_ref, decay_ref, angle_ref, packed_ref, weighted, stored):
     rows = grad_ref.shape[0]
     modes, width = decay_ref.shape
     weighted[...] = grad_ref[...].astype(jnp.float32) * gate_ref[...].astype(jnp.float32)
@@ -77,27 +78,16 @@
     sine, cosine = sine_cosine(angle)
     radius = jnp.exp(-decay)
     step_real, step_imaginary = radius * cosine, -radius * sine
-    span_sine, span_cosine = sine_cosine(angle * float(rows))
-    span_radius = jnp.exp(-decay * float(rows))
-    power_real, power_imaginary = span_radius * span_cosine, -span_radius * span_sine
-
-    def store_power(column):
-        def store(row, value):
-            power_ref[row : row + modes, column : column + LANES] = value
-
-        return store
-
-    pack_slices(power_real, power_real, store_power(0))
-    pack_slices(-power_imaginary, power_imaginary, store_power(LANES))
     parts = [[] for _ in range(6)]
     for first in range(0, modes, SUB):
         sr, si = step_real[first : first + SUB], step_imaginary[first : first + SUB]
 
         def block(j, carry, sr=sr, si=si):
             br, bi, lr, li, kr, ki = carry
+            last = rows - SUB - j * SUB
+            ws, ss, ups = line_block(weighted, last), line_block(stored, last), line_block(stored, j * SUB)
             for r in range(SUB):
-                t = rows - 1 - (j * SUB + r)
-                w, s, s_up = spread(weighted, t), spread(stored, t), spread(stored, j * SUB + r)
+                w, s, s_up = ws[SUB - 1 - r], ss[SUB - 1 - r], ups[r]
                 br, bi = (w + sr * br) - si * bi, sr * bi + si * br
                 lr, li = lr + s * br, li + s * bi
                 kr = kr + s_up
@@ -111,8 +101,8 @@
     whole = [jnp.concatenate(part, axis=0) for part in parts]
     for which in range(3):
 
-        def store(row, value, column=which * LANES):
-            packed_ref[row : row + modes, column : column + LANES] = value
+        def store(row, value, which=which):
+            packed_ref[pl.ds(3 * row + which, modes, stride=3), :] = value
 
         pack_slices(whole[2 * which], whole[2 * which + 1], store)
 
@@ -121,13 +111,26 @@
     return first * second_direct + pltpu.roll(first, HALF, 1) * second_cross
 
 
-def scan_kernel(where_ref, packed_ref, power_ref, out_ref):
-    rows = packed_ref.shape[0]
+def slice_values(ref, where):
+    modes, width = ref.shape
+    mode, block = lax.rem(where, modes), lax.div(where, modes)
+    chosen = jnp.zeros((modes, LANES), jnp.float32)
+    for tile in range(width // LANES):
+        chosen = jnp.where(lax.div(block, 2) == tile, ref[:, tile * LANES : (tile + 1) * LANES], chosen)
+    rows = lax.broadcasted_iota(jnp.int32, chosen.shape, 0)
+    line = jnp.sum(jnp.where(rows == mode, chosen, 0.0), axis=0, keepdims=True)
+    line = jnp.where(lane_low(line.shape) == (lax.rem(block, 2) == 0), line, 0.0)
+    return line + pltpu.roll(line, HALF, 1)
+
+
+def scan_kernel(span, where_ref, packed_ref, decay_ref, angle_ref, out_ref):
+    rows = packed_ref.shape[0] // 3
     low = lane_low((1, LANES))
-    mine = lax.broadcasted_iota(jnp.int32, power_ref.shape, 0) == where_ref[0]
-    power = jnp.sum(jnp.where(mine, power_ref[...], 0.0), axis=0, keepdims=True)
-    direct, cross = power[:, 0:LANES], power[:, LANES : 2 * LANES]
-    state = packed_ref[:, 0:LANES]
+    decay, angle = slice_values(decay_ref, where_ref[0]), slice_values(angle_ref, where_ref[0])
+    sine, cosine = sine_cosine(angle * float(span))
+    radius = jnp.exp(-decay * float(span))
+    direct, cross = radius * cosine, jnp.where(low, radius * sine, -radius * sine)
+    state = packed_ref[pl.ds(0, rows, stride=3), :]
     index = lax.broadcasted_iota(jnp.int32, (rows, LANES), 0)
 
     def from_later(value, shift):
@@ -137,24 +140,23 @@
     shift = 1
     while shift < rows:
         state = state + times(from_later(state, shift), direct, cross)
-        real = jnp.where(low, direct, pltpu.roll(direct, HALF, 1))
-        direct, cross = real * real - cross * cross, 2.0 * real * cross
+        direct, cross = direct * direct - cross * cross, 2.0 * direct * cross
         shift *= 2
-    sums = packed_ref[:, LANES : 2 * LANES]
-    reach = packed_ref[:, 2 * LANES : 3 * LANES]
+    sums = packed_ref[pl.ds(1, rows, stride=3), :]
+    reach = packed_ref[pl.ds(2, rows, stride=3), :]
     swapped = pltpu.roll(reach, HALF, 1)
     low_rows = lane_low((rows, LANES))
     reach_direct = jnp.where(low_rows, reach, swapped)
     reach_cross = jnp.where(low_rows, -swapped, reach)
     total = jnp.sum(sums + times(state, reach_direct, reach_cross), axis=0, keepdims=True)
-    out_ref[:, 0:LANES] = state
-    out_ref[:, LANES : 2 * LANES] = jnp.broadcast_to(total, (rows, LANES))
+    out_ref[pl.ds(0, rows, stride=2), :] = state
+    out_ref[pl.ds(1, rows, stride=2), :] = jnp.broadcast_to(total, (rows, LANES))
 
 
 def residue_kernel(back_ref, decay_ref, raw_ref, squares_ref):
     modes, width = decay_ref.shape
     scale = scale_of(decay_ref[...])
-    real, imaginary = unpack_slices(lambda row: back_ref[row : row + modes, LANES : 2 * LANES], modes, width)
+    real, imaginary = unpack_slices(lambda row: back_ref[pl.ds(2 * row + 1, modes, stride=2), :], modes, width)
     real, imaginary = real * scale, -(imaginary * scale)
     raw_ref[0] = real
     raw_ref[1] = imaginary
@@ -178,7 +180,7 @@
     step_real, step_imaginary = radius * cosine, -radius * sine
     scale = scale_of(decay)
     weight_real, weight_imaginary = residue_ref[0] * scale, residue_ref[1] * scale
-    real, imaginary = unpack_slices(lambda row: back_ref[row : row + modes, 0:LANES], modes, width)
+    real, imaginary = unpack_slices(lambda row: back_ref[pl.ds(2 * row, modes, stride=2), :], modes, width)
     start_real = weight_real * real - weight_imaginary * imaginary
     start_imaginary = weight_real * imaginary + weight_imaginary * real
     span = 2 * LANES
@@ -194,9 +196,11 @@
 
         def block(j, carry, steps=steps, cut=cut):
             carry = list(carry)
+            last = rows - SUB - j * SUB
+            ws = line_block(weighted, last, cut)
             for r in range(SUB):
-                t = rows - 1 - (j * SUB + r)
-                w = spread(weighted, t, cut)
+                t = last + SUB - 1 - r
+                w = ws[SUB - 1 - r]
                 total = None
                 for which, (sr, si, cr, ci) in enumerate(steps):
                     qr, qi = carry[2 * which], carry[2 * which + 1]
@@ -226,6 +230,11 @@
     out_ref[...] = raw_ref[...] * (clip_level / jnp.maximum(norm, clip_level))[None]
 
 
+def turn(array, parts):
+    sent = array.reshape(array.shape[0] // parts, parts * LANES)
+    return lax.all_to_all(sent, "seq", 0, 0, tiled=True).reshape(array.shape)
+
+
 def on_device(
     grad_out, gate_query, key_input, value_input, decay_rate, pole_angle, residue, skip_gain
 ):
@@ -233,24 +242,21 @@
     modes = decay_rate.shape[0]
     shards, chan_shards = lax.axis_size("seq"), lax.axis_size("chan")
     slices = modes * width // HALF
-    packed, power = pl.pallas_call(
+    packed = pl.pallas_call(
         local_kernel,
-        out_shape=(
-            jax.ShapeDtypeStruct((slices, 3 * LANES), jnp.float32),
-            jax.ShapeDtypeStruct((slices, 2 * LANES), jnp.float32),
-        ),
+        out_shape=jax.ShapeDtypeStruct((3 * slices, LANES), jnp.float32),
         scratch_shapes=[pltpu.VMEM((rows, width), jnp.float32)] * 2,
         name="local_pass",
     )(grad_out, gate_query, key_input, value_input, decay_rate, pole_angle)
-    turned = lax.all_to_all(packed, "seq", 0, 0, tiled=True)
+    turned = turn(packed, 3)
     where = lax.axis_index("seq").reshape(1)
     answers = pl.pallas_call(
-        scan_kernel,
-        in_specs=[pl.BlockSpec(memory_space=pltpu.SMEM)] + [pl.BlockSpec(memory_space=pltpu.VMEM)] * 2,
-        out_shape=jax.ShapeDtypeStruct((shards, 2 * LANES), jnp.float32),
+        functools.partial(scan_kernel, rows),
+        in_specs=[pl.BlockSpec(memory_space=pltpu.SMEM)] + [pl.BlockSpec(memory_space=pltpu.VMEM)] * 3,
+        out_shape=jax.ShapeDtypeStruct((2 * shards, LANES), jnp.float32),
         name="scan_shards",
-    )(where, turned, power)
-    back = lax.all_to_all(answers, "seq", 0, 0, tiled=True)
+    )(where, turned, decay_rate, pole_angle)
+    back = turn(answers, 2)
     raw, squares = pl.pallas_call(
         residue_kernel,
         out_shape=(

time: 98.1 us -> 96 us (0.979)
  local copies, waits for them, and re-layouts: 4.77 us -> 1.26 us
  blocking collectives: 23.9 us -> 25.4 us
    all_to_all x2 -> x0, local copies, waits for them, and re-layouts: 2.84 us -> none  [the longest x1 1.8 us: on_device(): turned = lax.all_to_all(packed, 'seq', 0, 0, tiled=True)]
    all_to_all x1, blocking collectives: 23.9 us -> 25.4 us  [turn(): return lax.all_to_all(sent, 'seq', 0, 0, tiled=True).reshape(array.shape)]
where the time goes in v2:
time: 96 us; the launch traced here: 94.8 us
  starting transfers between devices  30.9 us (32%)
  blocking collectives  25.4 us (26%)
  waiting for transfers between devices  22.4 us (23%)
  Pallas kernels  14.2 us (15%)
  local copies, waits for them, and re-layouts  1.26 us (1%)
    all_to_all x1, blocking collectives, turn(): return lax.all_to_all(sent, 'seq', 0, 0, tiled=True).reshape(array.shape)  25.4 us
    all_to_all x1, starting transfers between devices, turn(): return lax.all_to_all(sent, 'seq', 0, 0, tiled=True).reshape(array.shape)  24.1 us
    all_to_all x1, waiting for transfers between devices, turn(): return lax.all_to_all(sent, 'seq', 0, 0, tiled=True).reshape(array.shape)  20 us
    all_to_all x1, starting transfers between devices, on_device(): all_squares = lax.all_to_all(squares, 'chan', 0, 0, tiled=True)  6.82 us
    pallas_call x1, Pallas kernels, on_device(): pl.pallas_call(local_kernel, out_shape=jax.ShapeDtypeStruct((3 * slices,...  4.71 us
    pallas_call x1, Pallas kernels, on_device(): pl.pallas_call(signal_kernel, out_shape=(jax.ShapeDtypeStruct((rows, widt...  3.96 us
    all_to_all x1, waiting for transfers between devices, on_device(): all_squares = lax.all_to_all(squares, 'chan', 0, 0, tiled=True)  2.49 us
    pallas_call x1, Pallas kernels, on_device(): pl.pallas_call(functools.partial(scan_kernel, rows), in_specs=[pl.BlockSp...  2.27 us
  transfers between devices with their start and end apart: 2, of which 2 were waited for; matrix products, arithmetic and copies ran while one was open for 0% of the time, Pallas kernels for 4%

profile of v2, /device:TPU:1, one launch (start us, length us, event | category | flops | bytes accessed | tf_op | source)
XLA Modules:
  0.0 94.8 jit_solution(12058740233503476911)
XLA Ops:
  0.6 4.7 %local_pass.1 = f32[384,128]{1,0:T(8,128)} custom-call(bf16[128,512]{1,0:T(8,128)(2,1)} %grad_ref.3, bf16[128,512]{1,0:T(8,128)(2,1)} %gate_ref.3, bf16[128,512]{1,0:T(8,128)(2,1)} %key_ref.3, bf16[128,512]{1,0:T(8,128)(2,1)} %value_ref.3, f32[16,512]{1,0:T(8,128)} %decay_ref.7, f32[16,512]{1,0:T(8,128)} %angle_ref.5), custom_call_target="tpu_custom_call" | custom-call | tf_op jit(solution)/shard_map/local_pass/pallas_call | solution.py:245
  5.3 24.1 %all-to-all-start = ((f32[128,1,384]{2,1,0:T(1,128)}), f32[128,1,384]{2,1,0:T(1,128)S(1)}, u32[]{:S(2)}, u32[]{:S(2)}) async-start(f32[128,1,384]{2,1,0:T(1,128)} %bitcast.13), calls=%async_computation | async-start | bytes 393216 | tf_op jit(solution)/shard_map/all_to_all | solution.py:235
  29.4 20.0 %all-to-all-done = f32[128,1,384]{2,1,0:T(1,128)S(1)} async-done(((f32[128,1,384]{2,1,0:T(1,128)}), f32[128,1,384]{2,1,0:T(1,128)S(1)}, u32[]{:S(2)}, u32[]{:S(2)}) %all-to-all-start) | async-done | bytes 196640 | tf_op jit(solution)/shard_map/all_to_all | solution.py:235
  49.4 0.0 copy-start
  49.4 0.7 copy-done
  50.0 2.3 %scan_shards.1 = f32[256,128]{1,0:T(8,128)} custom-call(s32[1]{0:T(128)} %bitcast.where_ref, f32[384,128]{1,0:T(8,128)} %bitcast.12, f32[16,512]{1,0:T(8,128)} %decay_ref.7, f32[16,512]{1,0:T(8,128)} %angle_ref.5), custom_call_target="tpu_custom_call" | custom-call | tf_op jit(solution)/shard_map/scan_shards/pallas_call | solution.py:253
  52.3 25.4 %all_to_all.29 = f32[128,1,256]{2,1,0:T(1,128)} all-to-all(f32[128,1,256]{2,1,0:T(1,128)} %bitcast.14), channel_id=1, replica_groups=mesh['seq'=128,'chan'=8] {'seq'}, dimensions={0} | all-to-all | bytes 262144 | tf_op jit(solution)/shard_map/all_to_all | solution.py:235
  77.7 1.6 %residue_sums.1 = (f32[2,16,512]{2,1,0:T(8,128)}, f32[8,128]{1,0:T(8,128)}) custom-call(f32[256,128]{1,0:T(8,128)} %bitcast.10, f32[16,512]{1,0:T(8,128)} %decay_ref.7), custom_call_target="tpu_custom_call" | custom-call | tf_op jit(solution)/shard_map/residue_sums/pallas_call | solution.py:260
  79.3 6.8 %all-to-all-start.2 = ((f32[8,1,128]{2,1,0:T(1,128)}), f32[8,1,128]{2,1,0:T(1,128)S(1)}, u32[]{:S(2)}, u32[]{:S(2)}) async-start(f32[8,1,128]{2,1,0:T(1,128)} %bitcast.16), calls=%async_computation.2 | async-start | bytes 8192 | tf_op jit(solution)/shard_map/all_to_all | solution.py:268
  86.1 4.0 %signal_pass.1 = (bf16[128,512]{1,0:T(8,128)(2,1)}, bf16[128,512]{1,0:T(8,128)(2,1)}) custom-call(f32[256,128]{1,0:T(8,128)} %bitcast.11, bf16[128,512]{1,0:T(8,128)(2,1)} %grad_ref.3, bf16[128,512]{1,0:T(8,128)(2,1)} %gate_ref.3, bf16[128,512]{1,0:T(8,128)(2,1)} %key_ref.3, bf16[128,512]{1,0:T(8,128)(2,1)} %value_ref.3, f32[16,512]{1,0:T(8,128)} %decay_ref.7, ...), custom_call_target="tpu_custom_call" | custom-call | flops 20971520 | bytes 786432 | tf_op jit(solution)/shard_map/signal_pass/pallas_call | solution.py:269
  90.1 2.5 %all-to-all-done.2 = f32[8,1,128]{2,1,0:T(1,128)S(1)} async-done(((f32[8,1,128]{2,1,0:T(1,128)}), f32[8,1,128]{2,1,0:T(1,128)S(1)}, u32[]{:S(2)}, u32[]{:S(2)}) %all-to-all-start.2) | async-done | bytes 4128 | tf_op jit(solution)/shard_map/all_to_all | solution.py:268
  92.6 0.0 copy-start.1
  92.6 0.6 copy-done.1
  93.2 1.6 %clip.1 = f32[2,16,512]{2,1,0:T(8,128)} custom-call(f32[8,128]{1,0:T(8,128)} %bitcast.15, f32[2,16,512]{2,1,0:T(8,128)} %get-tuple-element.10.raw_ref), custom_call_target="tpu_custom_call" | custom-call | tf_op jit(solution)/shard_map/clip/pallas_call | solution.py:280
Async XLA Ops:
  5.3 44.0 %all-to-all-start = ((f32[128,1,384]{2,1,0:T(1,128)}), f32[128,1,384]{2,1,0:T(1,128)S(1)}, u32[]{:S(2)}, u32[]{:S(2)}) async-start(f32[128,1,384]{2,1,0:T(1,128)} %bitcast.13), calls=%async_computation | async-start | bytes 393216 | tf_op jit(solution)/shard_map/all_to_all | solution.py:235
  49.4 0.7 copy-start
  79.3 13.3 %all-to-all-start.2 = ((f32[8,1,128]{2,1,0:T(1,128)}), f32[8,1,128]{2,1,0:T(1,128)S(1)}, u32[]{:S(2)}, u32[]{:S(2)}) async-start(f32[8,1,128]{2,1,0:T(1,128)} %bitcast.16), calls=%async_computation.2 | async-start | bytes 8192 | tf_op jit(solution)/shard_map/all_to_all | solution.py:268
  92.6 0.6 copy-start.1

commit v3 on v2

--- a/solution.py
+++ b/solution.py
@@ -11,6 +11,9 @@
 LANES = 128
 HALF = 64
 SUB = 8
+CORES = 2
+CHIPS_Z = 16
+RUN = CORES * CHIPS_Z
 TURN_PARTS = (1.5703125, 4.837512969970703e-4, 7.54978995489188e-8)
 
 
@@ -50,23 +53,32 @@
 
 
 def pack_slices(real, imaginary, store):
-    modes, width = real.shape
-    low = lane_low((modes, LANES))
-    for tile in range(width // LANES):
+    low = lane_low((real.shape[0], LANES))
+    for tile in range(real.shape[1] // LANES):
         re = real[:, tile * LANES : (tile + 1) * LANES]
         im = imaginary[:, tile * LANES : (tile + 1) * LANES]
-        store(2 * tile * modes, jnp.where(low, re, pltpu.roll(im, HALF, 1)))
-        store((2 * tile + 1) * modes, jnp.where(low, pltpu.roll(re, HALF, 1), im))
+        store(2 * tile, jnp.where(low, re, pltpu.roll(im, HALF, 1)))
+        store(2 * tile + 1, jnp.where(low, pltpu.roll(re, HALF, 1), im))
 
 
 def unpack_slices(load, modes, width):
     low = lane_low((modes, LANES))
     reals, imaginaries = [], []
     for tile in range(width // LANES):
-        even, odd = load(2 * tile * modes), load((2 * tile + 1) * modes)
+        even, odd = load(2 * tile), load(2 * tile + 1)
         reals.append(jnp.where(low, even, pltpu.roll(odd, HALF, 1)))
         imaginaries.append(jnp.where(low, pltpu.roll(even, HALF, 1), odd))
     return jnp.concatenate(reals, axis=1), jnp.concatenate(imaginaries, axis=1)
+
+
+def answer_lines(back_ref, part, modes):
+    halves = modes // SUB
+
+    def load(block):
+        lines = [(block * halves + half) * 2 * SUB + part * SUB for half in range(halves)]
+        return jnp.concatenate([back_ref[first : first + SUB] for first in lines], axis=0)
+
+    return load
 
 
 def local_kernel(grad_ref, gate_ref, key_ref, value_ref, decay_ref, angle_ref, packed_ref, weighted, stored):
@@ -78,7 +90,6 @@
     sine, cosine = sine_cosine(angle)
     radius = jnp.exp(-decay)
     step_real, step_imaginary = radius * cosine, -radius * sine
-    parts = [[] for _ in range(6)]
     for first in range(0, modes, SUB):
         sr, si = step_real[first : first + SUB], step_imaginary[first : first + SUB]
 
@@ -96,67 +107,121 @@
 
         zero = jnp.zeros((SUB, width), jnp.float32)
         done = lax.fori_loop(0, rows // SUB, block, (zero,) * 6)
-        for part, value in zip(parts, done):
-            part.append(value)
-    whole = [jnp.concatenate(part, axis=0) for part in parts]
-    for which in range(3):
-
-        def store(row, value, which=which):
-            packed_ref[pl.ds(3 * row + which, modes, stride=3), :] = value
-
-        pack_slices(whole[2 * which], whole[2 * which + 1], store)
-
-
-def times(first, second_direct, second_cross):
-    return first * second_direct + pltpu.roll(first, HALF, 1) * second_cross
-
-
-def slice_values(ref, where):
+        for part in range(3):
+
+            def store(block, value, part=part, half=first // SUB):
+                line = (block * (modes // SUB) + half) * 3 * SUB + part * SUB
+                packed_ref[line : line + SUB] = value
+
+            pack_slices(done[2 * part], done[2 * part + 1], store)
+
+
+def swap(value):
+    return pltpu.roll(value, HALF, 1)
+
+
+def factors(value, swapped):
+    low = lane_low(value.shape)
+    return jnp.where(low, value, swapped), jnp.where(low, -swapped, value)
+
+
+def step(added, state, power):
+    direct, cross = power
+    here, there = state
+    return added[0] + (here * direct + there * cross), added[1] + (there * direct - here * cross)
+
+
+def squared(power):
+    direct, cross = power
+    return direct * direct - cross * cross, 2.0 * direct * cross
+
+
+def place_of(where_ref):
+    where = where_ref[0]
+    return lax.div(where, RUN), lax.rem(lax.div(where, CORES), CHIPS_Z), lax.rem(where, CORES)
+
+
+def slice_values(ref, chip):
     modes, width = ref.shape
-    mode, block = lax.rem(where, modes), lax.div(where, modes)
-    chosen = jnp.zeros((modes, LANES), jnp.float32)
+    halves = modes // SUB
+    block, half = lax.div(chip, halves), lax.rem(chip, halves)
+    chosen = jnp.zeros((SUB, LANES), jnp.float32)
     for tile in range(width // LANES):
-        chosen = jnp.where(lax.div(block, 2) == tile, ref[:, tile * LANES : (tile + 1) * LANES], chosen)
-    rows = lax.broadcasted_iota(jnp.int32, chosen.shape, 0)
-    line = jnp.sum(jnp.where(rows == mode, chosen, 0.0), axis=0, keepdims=True)
-    line = jnp.where(lane_low(line.shape) == (lax.rem(block, 2) == 0), line, 0.0)
-    return line + pltpu.roll(line, HALF, 1)
-
-
-def scan_kernel(span, where_ref, packed_ref, decay_ref, angle_ref, out_ref):
-    rows = packed_ref.shape[0] // 3
-    low = lane_low((1, LANES))
-    decay, angle = slice_values(decay_ref, where_ref[0]), slice_values(angle_ref, where_ref[0])
+        for first in range(halves):
+            here = (lax.div(block, 2) == tile) & (half == first)
+            part = ref[first * SUB : (first + 1) * SUB, tile * LANES : (tile + 1) * LANES]
+            chosen = jnp.where(here, part, chosen)
+    chosen = jnp.where(lane_low(chosen.shape) == (lax.rem(block, 2) == 0), chosen, 0.0)
+    return chosen + swap(chosen)
+
+
+def span_power(span, decay_ref, angle_ref, chip):
+    decay, angle = slice_values(decay_ref, chip), slice_values(angle_ref, chip)
     sine, cosine = sine_cosine(angle * float(span))
     radius = jnp.exp(-decay * float(span))
-    direct, cross = radius * cosine, jnp.where(low, radius * sine, -radius * sine)
-    state = packed_ref[pl.ds(0, rows, stride=3), :]
-    index = lax.broadcasted_iota(jnp.int32, (rows, LANES), 0)
-
-    def from_later(value, shift):
-        return jnp.where(index < rows - shift, pltpu.roll(value, rows - shift, 0), 0.0)
-
-    state = from_later(state, 1)
-    shift = 1
-    while shift < rows:
-        state = state + times(from_later(state, shift), direct, cross)
-        direct, cross = direct * direct - cross * cross, 2.0 * direct * cross
-        shift *= 2
-    sums = packed_ref[pl.ds(1, rows, stride=3), :]
-    reach = packed_ref[pl.ds(2, rows, stride=3), :]
-    swapped = pltpu.roll(reach, HALF, 1)
-    low_rows = lane_low((rows, LANES))
-    reach_direct = jnp.where(low_rows, reach, swapped)
-    reach_cross = jnp.where(low_rows, -swapped, reach)
-    total = jnp.sum(sums + times(state, reach_direct, reach_cross), axis=0, keepdims=True)
-    out_ref[pl.ds(0, rows, stride=2), :] = state
-    out_ref[pl.ds(1, rows, stride=2), :] = jnp.broadcast_to(total, (rows, LANES))
+    return radius * cosine, jnp.where(lane_low(sine.shape), radius * sine, -radius * sine)
+
+
+def run_kernel(span, where_ref, own_ref, other_ref, decay_ref, angle_ref, message_ref, inside_ref):
+    _, chip, core = place_of(where_ref)
+    power = span_power(span, decay_ref, angle_ref, chip)
+    first_core = core == 0
+
+    def tiles(part, z):
+        line = (3 * z + part) * SUB
+        own, other = own_ref[line : line + SUB], other_ref[line : line + SUB]
+        pair = jnp.where(first_core, own, other), jnp.where(first_core, other, own)
+        return [(value, swap(value)) for value in pair]
+
+    zero = jnp.zeros((SUB, LANES), jnp.float32)
+    state, total, reach = (zero, zero), zero, (zero, zero)
+    for z in range(CHIPS_Z):
+        for value in tiles(2, z):
+            reach = step(value, reach, power)
+    for z in reversed(range(CHIPS_Z)):
+        carries, sums, reaches = tiles(0, z), tiles(1, z), tiles(2, z)
+        inside = []
+        for c in reversed(range(CORES)):
+            inside.append(state[0])
+            direct, cross = factors(*reaches[c])
+            total = total + (sums[c][0] + (state[0] * direct + state[1] * cross))
+            state = step(carries[c], state, power)
+        inside_ref[z * SUB : (z + 1) * SUB] = jnp.where(first_core, inside[1], inside[0])
+    copies = message_ref.shape[0] // (3 * SUB)
+    for copy in range(copies):
+        for part, value in enumerate((state[0], total, reach[0])):
+            line = (3 * copy + part) * SUB
+            message_ref[line : line + SUB] = value
+
+
+def answer_kernel(span, where_ref, message_ref, inside_ref, decay_ref, angle_ref, out_ref):
+    mine, chip, core = place_of(where_ref)
+    power = span_power(span, decay_ref, angle_ref, chip)
+    run_power = power
+    for _ in range(RUN.bit_length() - 1):
+        run_power = squared(run_power)
+    zero = jnp.zeros((SUB, LANES), jnp.float32)
+    state, total = (zero, zero), zero
+    entering = (zero, zero)
+    for x in reversed(range(message_ref.shape[0] // (3 * SUB))):
+        carry, sums, reach = [message_ref[(3 * x + part) * SUB : (3 * x + part + 1) * SUB] for part in range(3)]
+        entering = tuple(jnp.where(mine == x, new, old) for new, old in zip(state, entering))
+        direct, cross = factors(reach, swap(reach))
+        total = total + (sums + (state[0] * direct + state[1] * cross))
+        state = step((carry, swap(carry)), state, run_power)
+    moved = step((zero, zero), entering, power)
+    entering = tuple(jnp.where(core == CORES - 1, here, there) for here, there in zip(entering, moved))
+    chip_power = squared(power)
+    for z in reversed(range(CHIPS_Z)):
+        out_ref[2 * z * SUB : (2 * z + 1) * SUB] = inside_ref[z * SUB : (z + 1) * SUB] + entering[0]
+        out_ref[(2 * z + 1) * SUB : (2 * z + 2) * SUB] = total
+        entering = step((zero, zero), entering, chip_power)
 
 
 def residue_kernel(back_ref, decay_ref, raw_ref, squares_ref):
     modes, width = decay_ref.shape
     scale = scale_of(decay_ref[...])
-    real, imaginary = unpack_slices(lambda row: back_ref[pl.ds(2 * row + 1, modes, stride=2), :], modes, width)
+    real, imaginary = unpack_slices(answer_lines(back_ref, 1, modes), modes, width)
     real, imaginary = real * scale, -(imaginary * scale)
     raw_ref[0] = real
     raw_ref[1] = imaginary
@@ -180,7 +245,7 @@
     step_real, step_imaginary = radius * cosine, -radius * sine
     scale = scale_of(decay)
     weight_real, weight_imaginary = residue_ref[0] * scale, residue_ref[1] * scale
-    real, imaginary = unpack_slices(lambda row: back_ref[pl.ds(2 * row, modes, stride=2), :], modes, width)
+    real, imaginary = unpack_slices(answer_lines(back_ref, 0, modes), modes, width)
     start_real = weight_real * real - weight_imaginary * imaginary
     start_imaginary = weight_real * imaginary + weight_imaginary * real
     span = 2 * LANES
@@ -230,9 +295,19 @@
     out_ref[...] = raw_ref[...] * (clip_level / jnp.maximum(norm, clip_level))[None]
 
 
-def turn(array, parts):
-    sent = array.reshape(array.shape[0] // parts, parts * LANES)
-    return lax.all_to_all(sent, "seq", 0, 0, tiled=True).reshape(array.shape)
+def on_chip(*shape):
+    return pltpu.VMEM(shape, jnp.float32)
+
+
+def kept(array):
+    return pltpu.with_memory_space_constraint(array, pltpu.VMEM)
+
+
+def groups(shards):
+    runs = shards // RUN
+    along_z = [[x * RUN + z * CORES + c for z in range(CHIPS_Z)] for x in range(runs) for c in range(CORES)]
+    along_x = [[x * RUN + inner for x in range(runs)] for inner in range(RUN)]
+    return along_z, along_x
 
 
 def on_device(
@@ -242,30 +317,41 @@
     modes = decay_rate.shape[0]
     shards, chan_shards = lax.axis_size("seq"), lax.axis_size("chan")
     slices = modes * width // HALF
+    along_z, along_x = groups(shards)
+    where, grad_out = lax.optimization_barrier((lax.axis_index("seq").reshape(1), grad_out))
+    scalar = [pl.BlockSpec(memory_space=pltpu.SMEM)]
+    whole = pl.BlockSpec(memory_space=pltpu.VMEM)
     packed = pl.pallas_call(
         local_kernel,
-        out_shape=jax.ShapeDtypeStruct((3 * slices, LANES), jnp.float32),
+        out_shape=on_chip(3 * slices, LANES),
         scratch_shapes=[pltpu.VMEM((rows, width), jnp.float32)] * 2,
         name="local_pass",
     )(grad_out, gate_query, key_input, value_input, decay_rate, pole_angle)
-    turned = turn(packed, 3)
-    where = lax.axis_index("seq").reshape(1)
+    own = lax.all_to_all(packed, "seq", 0, 0, tiled=True, axis_index_groups=along_z)
+    other = lax.ppermute(own, "seq", [(shard, shard ^ 1) for shard in range(shards)])
+    message, inside = pl.pallas_call(
+        functools.partial(run_kernel, rows),
+        in_specs=scalar + [whole] * 4,
+        out_shape=(on_chip(3 * SUB * (shards // RUN), LANES), on_chip(CHIPS_Z * SUB, LANES)),
+        name="join_run",
+    )(where, kept(own), kept(other), decay_rate, pole_angle)
+    message = lax.all_to_all(message, "seq", 0, 0, tiled=True, axis_index_groups=along_x)
     answers = pl.pallas_call(
-        functools.partial(scan_kernel, rows),
-        in_specs=[pl.BlockSpec(memory_space=pltpu.SMEM)] + [pl.BlockSpec(memory_space=pltpu.VMEM)] * 3,
-        out_shape=jax.ShapeDtypeStruct((2 * shards, LANES), jnp.float32),
-        name="scan_shards",
-    )(where, turned, decay_rate, pole_angle)
-    back = turn(answers, 2)
+        functools.partial(answer_kernel, rows),
+        in_specs=scalar + [whole] * 4,
+        out_shape=on_chip(2 * CHIPS_Z * SUB, LANES),
+        name="join_runs",
+    )(where, kept(message), kept(inside), decay_rate, pole_angle)
+    back = kept(lax.all_to_all(answers, "seq", 0, 0, tiled=True, axis_index_groups=along_z))
     raw, squares = pl.pallas_call(
         residue_kernel,
         out_shape=(
-            jax.ShapeDtypeStruct((2, modes, width), jnp.float32),
-            jax.ShapeDtypeStruct((chan_shards, LANES), jnp.float32),
+            on_chip(2, modes, width),
+            on_chip(chan_shards, LANES),
         ),
         name="residue_sums",
     )(back, decay_rate)
-    all_squares = lax.all_to_all(squares, "chan", 0, 0, tiled=True)
+    all_squares = kept(lax.all_to_all(squares, "chan", 0, 0, tiled=True))
     grad_key, grad_value = pl.pallas_call(
         signal_kernel,
         out_shape=(jax.ShapeDtypeStruct((rows, width), jnp.bfloat16),) * 2,
@@ -281,7 +367,7 @@
         functools.partial(clip_kernel, clip_level),
         out_shape=jax.ShapeDtypeStruct((2, modes, width), jnp.float32),
         name="clip",
-    )(all_squares, raw)
+    )(all_squares, kept(raw))
     return (grad_key, grad_value, grad_residue)
 
 

time: 96 us -> 90 us (0.938)
  the two profiles are of different devices: /device:TPU:1 before, /device:TPU:2 now
where the time goes in v3:
time: 90 us; the launch traced here: 89.4 us
  blocking collectives  62.5 us (69%)
  Pallas kernels  12.1 us (13%)
  starting transfers between devices  9.01 us (10%)
  waiting for transfers between devices  5.13 us (6%)
    all_to_all x1, blocking collectives, on_device(): lax.all_to_all(packed, 'seq', 0, 0, tiled=True, axis_index_groups=along_z)  35.1 us
    all_to_all x1, blocking collectives, on_device(): lax.all_to_all(answers, 'seq', 0, 0, tiled=True, axis_index_groups=along_z)  18.7 us
    all_to_all x1, blocking collectives, on_device(): lax.all_to_all(message, 'seq', 0, 0, tiled=True, axis_index_groups=along_x)  8.71 us
    all_to_all x1, starting transfers between devices, on_device(): all_squares = kept(lax.all_to_all(squares, 'chan', 0, 0, tiled=True))  7.1 us
    pallas_call x1, Pallas kernels, on_device(): pl.pallas_call(local_kernel, out_shape=on_chip(3 * slices, LANES), scratc...  4.11 us
    pallas_call x1, Pallas kernels, on_device(): pl.pallas_call(signal_kernel, out_shape=(jax.ShapeDtypeStruct((rows, widt...  3.88 us
    all_to_all x1, waiting for transfers between devices, on_device(): all_squares = kept(lax.all_to_all(squares, 'chan', 0, 0, tiled=True))  3.72 us
    ppermute x1, starting transfers between devices, on_device(): lax.ppermute(own, 'seq', [(shard, shard ^ 1) for shard in range(shards)])  1.91 us
  transfers between devices with their start and end apart: 2, of which 2 were waited for; matrix products, arithmetic and copies ran while one was open for 0% of the time, Pallas kernels for 4%

profile of v3, /device:TPU:2, one launch (start us, length us, event | category | flops | bytes accessed | tf_op | source)
XLA Modules:
  0.0 89.4 jit_solution(12418581866945233725)
XLA Ops:
  0.6 4.1 %local_pass.1 = f32[384,128]{1,0:T(8,128)S(1)} custom-call(bf16[128,512]{1,0:T(8,128)(2,1)} %grad_ref.1, bf16[128,512]{1,0:T(8,128)(2,1)} %gate_ref.3, bf16[128,512]{1,0:T(8,128)(2,1)} %key_ref.3, bf16[128,512]{1,0:T(8,128)(2,1)} %value_ref.3, f32[16,512]{1,0:T(8,128)} %decay_ref.9, f32[16,512]{1,0:T(8,128)} %angle_ref.7), custom_call_target="tpu_custom_call" | custom-call | tf_op jit(solution)/shard_map/local_pass/pallas_call | solution.py:324
  4.8 35.1 %all_to_all.44 = f32[16,24,128]{2,1,0:T(8,128)S(1)} all-to-all(f32[16,24,128]{2,1,0:T(8,128)S(1)} %bitcast.16), channel_id=1, replica_groups={{0,16,32,48,64,80,96,112,128,144,160,176,192,208,224,240},{8,24,40,56,7..., dimensions={0} | all-to-all | bytes 393216 | tf_op jit(solution)/shard_map/all_to_all | solution.py:330
  39.9 1.9 %collective-permute-start = (f32[384,128]{1,0:T(8,128)S(1)}, f32[384,128]{1,0:T(8,128)S(1)}, u32[]{:S(2)}, u32[]{:S(2)}) collective-permute-start(f32[384,128]{1,0:T(8,128)S(1)} %bitcast.14), channel_id=1, source_target_pairs={{0,8},{8,0},{16,24},{24,16},{32,40},{40,32},{48,56},{56,48},{64,72... | collective-permute-start | bytes 589832 | tf_op jit(solution)/shard_map/ppermute | solution.py:331
  41.8 1.4 %collective-permute-done.other_ref = f32[384,128]{1,0:T(8,128)S(1)} collective-permute-done((f32[384,128]{1,0:T(8,128)S(1)}, f32[384,128]{1,0:T(8,128)S(1)}, u32[]{:S(2)}, u32[]{:S(2)}) %collective-permute-start) | collective-permute-done | bytes 196640 | tf_op jit(solution)/shard_map/ppermute | solution.py:331
  43.2 1.0 %join_run.1 = (f32[96,128]{1,0:T(8,128)S(1)}, f32[128,128]{1,0:T(8,128)S(1)}) custom-call(s32[1]{0:T(128)} %bitcast.where_ref, f32[384,128]{1,0:T(8,128)S(1)} %bitcast.15, f32[384,128]{1,0:T(8,128)S(1)} %collective-permute-done.other_ref, f32[16,512]{1,0:T(8,128)} %decay_ref.9, f32[16,512]{1,0:T(8,128)} %angle_ref.7), custom_call_target="tpu_custom_call" | custom-call | tf_op jit(solution)/shard_map/join_run/pallas_call | solution.py:332
  44.2 8.7 %all_to_all.45 = f32[4,24,128]{2,1,0:T(8,128)S(1)} all-to-all(f32[4,24,128]{2,1,0:T(8,128)S(1)} %bitcast.19), channel_id=1, replica_groups={{0,256,512,768},{8,264,520,776},{16,272,528,784},{24,280,536,792},{32,2..., dimensions={0} | all-to-all | bytes 98304 | tf_op jit(solution)/shard_map/all_to_all | solution.py:338
  52.9 0.9 %join_runs.1 = f32[256,128]{1,0:T(8,128)S(1)} custom-call(s32[1]{0:T(128)} %bitcast.where_ref, f32[96,128]{1,0:T(8,128)S(1)} %bitcast.18, f32[128,128]{1,0:T(8,128)S(1)} %get-tuple-element.14.inside_ref, f32[16,512]{1,0:T(8,128)} %decay_ref.9, f32[16,512]{1,0:T(8,128)} %angle_ref.7), custom_call_target="tpu_custom_call" | custom-call | tf_op jit(solution)/shard_map/join_runs/pallas_call | solution.py:339
  53.8 18.7 %all_to_all.46 = f32[16,16,128]{2,1,0:T(8,128)S(1)} all-to-all(f32[16,16,128]{2,1,0:T(8,128)S(1)} %bitcast.17), channel_id=1, replica_groups={{0,16,32,48,64,80,96,112,128,144,160,176,192,208,224,240},{8,24,40,56,7..., dimensions={0} | all-to-all | bytes 262144 | tf_op jit(solution)/shard_map/all_to_all | solution.py:345
  72.5 1.4 %residue_sums.1 = (f32[2,16,512]{2,1,0:T(8,128)S(1)}, f32[8,128]{1,0:T(8,128)}) custom-call(f32[256,128]{1,0:T(8,128)S(1)} %bitcast.12, f32[16,512]{1,0:T(8,128)} %decay_ref.9), custom_call_target="tpu_custom_call" | custom-call | tf_op jit(solution)/shard_map/residue_sums/pallas_call | solution.py:346
  73.9 7.1 %all-to-all-start.3 = ((f32[8,1,128]{2,1,0:T(1,128)}), f32[8,1,128]{2,1,0:T(1,128)S(1)}, u32[]{:S(2)}, u32[]{:S(2)}) async-start(f32[8,1,128]{2,1,0:T(1,128)} %bitcast.9), calls=%async_computation.3 | async-start | bytes 8192 | tf_op jit(solution)/shard_map/all_to_all | solution.py:354
  81.0 3.9 %signal_pass.1 = (bf16[128,512]{1,0:T(8,128)(2,1)}, bf16[128,512]{1,0:T(8,128)(2,1)}) custom-call(f32[256,128]{1,0:T(8,128)S(1)} %bitcast.13, bf16[128,512]{1,0:T(8,128)(2,1)} %grad_ref.1, bf16[128,512]{1,0:T(8,128)(2,1)} %gate_ref.3, bf16[128,512]{1,0:T(8,128)(2,1)} %key_ref.3, bf16[128,512]{1,0:T(8,128)(2,1)} %value_ref.3, f32[16,512]{1,0:T(8,128)} %decay_ref.9, ...), custom_call_target="tpu_custom_call" | custom-call | flops 20971520 | bytes 786432 | tf_op jit(solution)/shard_map/signal_pass/pallas_call | solution.py:355
  84.9 3.7 %all-to-all-done.3 = f32[8,1,128]{2,1,0:T(1,128)S(1)} async-done(((f32[8,1,128]{2,1,0:T(1,128)}), f32[8,1,128]{2,1,0:T(1,128)S(1)}, u32[]{:S(2)}, u32[]{:S(2)}) %all-to-all-start.3) | async-done | bytes 4128 | tf_op jit(solution)/shard_map/all_to_all | solution.py:354
  88.6 0.8 clip.1
Async XLA Ops:
  39.9 3.3 %collective-permute-start = (f32[384,128]{1,0:T(8,128)S(1)}, f32[384,128]{1,0:T(8,128)S(1)}, u32[]{:S(2)}, u32[]{:S(2)}) collective-permute-start(f32[384,128]{1,0:T(8,128)S(1)} %bitcast.14), channel_id=1, source_target_pairs={{0,8},{8,0},{16,24},{24,16},{32,40},{40,32},{48,56},{56,48},{64,72... | collective-permute-start | bytes 589832 | tf_op jit(solution)/shard_map/ppermute | solution.py:331
  73.9 14.7 %all-to-all-start.3 = ((f32[8,1,128]{2,1,0:T(1,128)}), f32[8,1,128]{2,1,0:T(1,128)S(1)}, u32[]{:S(2)}, u32[]{:S(2)}) async-start(f32[8,1,128]{2,1,0:T(1,128)} %bitcast.9), calls=%async_computation.3 | async-start | bytes 8192 | tf_op jit(solution)/shard_map/all_to_all | solution.py:354

commit v4 on v3

--- a/solution.py
+++ b/solution.py
@@ -81,39 +81,102 @@
     return load
 
 
-def local_kernel(grad_ref, gate_ref, key_ref, value_ref, decay_ref, angle_ref, packed_ref, weighted, stored):
+def product(first, second):
+    return first[0] * second[0] - first[1] * second[1], first[0] * second[1] + first[1] * second[0]
+
+
+def added_product(total, first, second):
+    return (
+        (total[0] + first[0] * second[0]) - first[1] * second[1],
+        (total[1] + first[0] * second[1]) + first[1] * second[0],
+    )
+
+
+def local_kernel(
+    grad_ref, gate_ref, key_ref, value_ref, decay_ref, angle_ref,
+    packed_ref, weighted, chunk_ref, power_ref, scale_ref, stored,
+):
     rows = grad_ref.shape[0]
     modes, width = decay_ref.shape
     weighted[...] = grad_ref[...].astype(jnp.float32) * gate_ref[...].astype(jnp.float32)
     stored[...] = key_ref[...].astype(jnp.float32) * value_ref[...].astype(jnp.float32)
-    decay, angle = decay_ref[...], angle_ref[...]
-    sine, cosine = sine_cosine(angle)
+    decay = decay_ref[...]
+    sine, cosine = sine_cosine(angle_ref[...])
     radius = jnp.exp(-decay)
-    step_real, step_imaginary = radius * cosine, -radius * sine
+    base = (radius * cosine, -radius * sine)
+    powers = [base]
+    for k in range(2, SUB + 1):
+        powers.append(product(powers[k // 2 - 1], powers[k - k // 2 - 1]))
+    for k in range(SUB):
+        power_ref[2 * k] = powers[k][0]
+        power_ref[2 * k + 1] = powers[k][1]
+    scale = scale_of(decay)
+    scale_ref[...] = scale
+    lags = []
+    for tile in range(width // LANES):
+        cut = slice(tile * LANES, (tile + 1) * LANES)
+
+        def lag_block(j, totals, cut=cut):
+            place = pl.ds(pl.multiple_of(j * SUB, SUB), SUB)
+            w, s = weighted[place, cut], stored[place, cut]
+            return tuple(
+                total + s * (w if lag == 0 else pltpu.roll(w, SUB - lag, 0)) for lag, total in enumerate(totals)
+            )
+
+        zero = jnp.zeros((SUB, LANES), jnp.float32)
+        lags.append(lax.fori_loop(0, rows // SUB, lag_block, (zero,) * SUB, unroll=4))
+    place = lax.broadcasted_iota(jnp.int32, (SUB, width), 0)
+    lag_sums = []
+    for lag in range(SUB):
+        line = jnp.concatenate([totals[lag] for totals in lags], axis=1)
+        line = jnp.sum(jnp.where(place < SUB - lag, line, 0.0), axis=0, keepdims=True)
+        lag_sums.append(jnp.broadcast_to(line, (SUB, width)))
     for first in range(0, modes, SUB):
-        sr, si = step_real[first : first + SUB], step_imaginary[first : first + SUB]
-
-        def block(j, carry, sr=sr, si=si):
-            br, bi, lr, li, kr, ki = carry
-            last = rows - SUB - j * SUB
-            ws, ss, ups = line_block(weighted, last), line_block(stored, last), line_block(stored, j * SUB)
-            for r in range(SUB):
-                w, s, s_up = ws[SUB - 1 - r], ss[SUB - 1 - r], ups[r]
-                br, bi = (w + sr * br) - si * bi, sr * bi + si * br
-                lr, li = lr + s * br, li + s * bi
-                kr = kr + s_up
-                kr, ki = sr * kr - si * ki, sr * ki + si * kr
-            return br, bi, lr, li, kr, ki
+        part_rows = slice(first, first + SUB)
+
+        def power(k, part_rows=part_rows):
+            return power_ref[2 * k - 2, part_rows], power_ref[2 * k - 1, part_rows]
+
+        def block(i, carry, power=power, part_rows=part_rows):
+            state, total, reach, far = carry
+            j = rows // SUB - 1 - i
+            ws, ss = line_block(weighted, j * SUB), line_block(stored, j * SUB)
+            eighth = power(SUB)
+            chunk_real, chunk_imaginary = ws[0], None
+            answer_real, answer_imaginary = ss[0] * eighth[0], ss[0] * eighth[1]
+            for k in range(1, SUB):
+                real, imaginary = power(k)
+                chunk_real = chunk_real + ws[k] * real
+                cross = ws[k] * imaginary
+                chunk_imaginary = cross if chunk_imaginary is None else chunk_imaginary + cross
+                answer_real = answer_real + ss[SUB - k] * real
+                answer_imaginary = answer_imaginary + ss[SUB - k] * imaginary
+            chunk, answer = (chunk_real, chunk_imaginary), (answer_real, answer_imaginary)
+            chunk_ref[2 * j, part_rows] = chunk_real
+            chunk_ref[2 * j + 1, part_rows] = chunk_imaginary
+            total = added_product(total, answer, state)
+            reach = added_product(reach, answer, far)
+            return added_product(chunk, eighth, state), total, reach, product(far, eighth)
 
         zero = jnp.zeros((SUB, width), jnp.float32)
-        done = lax.fori_loop(0, rows // SUB, block, (zero,) * 6)
-        for part in range(3):
+        pair = (zero, zero)
+        state, total, reach, _ = lax.fori_loop(
+            0, rows // SUB, block, (pair, pair, pair, (jnp.ones((SUB, width), jnp.float32), zero))
+        )
+        total = total[0] + lag_sums[0], total[1]
+        for lag in range(1, SUB):
+            real, imaginary = power(lag)
+            total = total[0] + lag_sums[lag] * real, total[1] + lag_sums[lag] * imaginary
+        own = scale[part_rows]
+        total = total[0] * own, total[1] * own
+        reach = reach[0] * own, reach[1] * own
+        for part, value in enumerate((state, total, reach)):
 
             def store(block, value, part=part, half=first // SUB):
                 line = (block * (modes // SUB) + half) * 3 * SUB + part * SUB
                 packed_ref[line : line + SUB] = value
 
-            pack_slices(done[2 * part], done[2 * part + 1], store)
+            pack_slices(value[0], value[1], store)
 
 
 def swap(value):
@@ -218,13 +281,11 @@
         entering = step((zero, zero), entering, chip_power)
 
 
-def residue_kernel(back_ref, decay_ref, raw_ref, squares_ref):
-    modes, width = decay_ref.shape
-    scale = scale_of(decay_ref[...])
+def residue_kernel(back_ref, raw_ref, squares_ref):
+    _, modes, width = raw_ref.shape
     real, imaginary = unpack_slices(answer_lines(back_ref, 1, modes), modes, width)
-    real, imaginary = real * scale, -(imaginary * scale)
     raw_ref[0] = real
-    raw_ref[1] = imaginary
+    raw_ref[1] = -imaginary
     squares = jnp.sum(real * real + imaginary * imaginary, axis=0, keepdims=True)
     total = squares[:, 0:LANES]
     for tile in range(1, width // LANES):
@@ -233,61 +294,69 @@
 
 
 def signal_kernel(
-    back_ref, grad_ref, gate_ref, key_ref, value_ref, decay_ref, angle_ref, residue_ref, skip_ref,
-    grad_key_ref, grad_value_ref, weighted, signal,
+    back_ref, weighted, chunk_ref, power_ref, scale_ref, key_ref, value_ref, residue_ref, skip_ref,
+    grad_key_ref, grad_value_ref, signal,
 ):
-    rows = grad_ref.shape[0]
-    modes, width = decay_ref.shape
-    weighted[...] = grad_ref[...].astype(jnp.float32) * gate_ref[...].astype(jnp.float32)
-    decay = decay_ref[...]
-    sine, cosine = sine_cosine(angle_ref[...])
-    radius = jnp.exp(-decay)
-    step_real, step_imaginary = radius * cosine, -radius * sine
-    scale = scale_of(decay)
-    weight_real, weight_imaginary = residue_ref[0] * scale, residue_ref[1] * scale
-    real, imaginary = unpack_slices(answer_lines(back_ref, 0, modes), modes, width)
-    start_real = weight_real * real - weight_imaginary * imaginary
-    start_imaginary = weight_real * imaginary + weight_imaginary * real
+    rows, width = weighted.shape
+    modes = scale_ref.shape[0]
+    scale = scale_ref[...]
+    weight = residue_ref[0] * scale, residue_ref[1] * scale
+    place = lax.broadcasted_iota(jnp.int32, (SUB, width), 0)
+    taps = []
+    for lag in range(SUB):
+        if lag:
+            tap = weight[0] * power_ref[2 * lag - 2] - weight[1] * power_ref[2 * lag - 1]
+        else:
+            tap = weight[0]
+        line = jnp.broadcast_to(jnp.sum(tap, axis=0, keepdims=True), (SUB, width))
+        taps.append(jnp.where(place < SUB - lag, line, 0.0))
+    taps[0] = taps[0] + skip_ref[...]
+    begin = product(weight, unpack_slices(answer_lines(back_ref, 0, modes), modes, width))
     span = 2 * LANES
     for column in range(0, width, span):
         cut = slice(column, column + span)
-        steps = [
-            tuple(a[first : first + SUB, cut] for a in (step_real, step_imaginary, weight_real, weight_imaginary))
-            for first in range(0, modes, SUB)
-        ]
-        begin = tuple(
-            a[first : first + SUB, cut] for first in range(0, modes, SUB) for a in (start_real, start_imaginary)
-        )
-
-        def block(j, carry, steps=steps, cut=cut):
-            carry = list(carry)
-            last = rows - SUB - j * SUB
-            ws = line_block(weighted, last, cut)
+        halves = [slice(first, first + SUB) for first in range(0, modes, SUB)]
+        scaled = [tuple(part[half, cut] for part in weight) for half in halves]
+        start = tuple(tuple(part[half, cut] for part in begin) for half in halves)
+
+        def block(i, states, cut=cut, halves=halves, scaled=scaled):
+            j = rows // SUB - 1 - i
             for r in range(SUB):
-                t = last + SUB - 1 - r
-                w = ws[SUB - 1 - r]
+                k = SUB - r
                 total = None
-                for which, (sr, si, cr, ci) in enumerate(steps):
-                    qr, qi = carry[2 * which], carry[2 * which + 1]
-                    qr, qi = (cr * w + sr * qr) - si * qi, (ci * w + sr * qi) + si * qr
-                    carry[2 * which], carry[2 * which + 1] = qr, qi
-                    total = qr if total is None else total + qr
-                place = pl.ds(pl.multiple_of(t * SUB, SUB), SUB)
+                for half, state in zip(halves, states):
+                    part = power_ref[2 * k - 2, half, cut] * state[0] - power_ref[2 * k - 1, half, cut] * state[1]
+                    total = part if total is None else total + part
+                line = pl.ds(pl.multiple_of((j * SUB + r) * SUB, SUB), SUB)
                 for part in range(span // LANES):
                     view = signal.at[cut.start // LANES + part]
-                    view[place, :] = total[:, part * LANES : (part + 1) * LANES]
-            return tuple(carry)
-
-        lax.fori_loop(0, rows // SUB, block, begin)
-    summed = skip_ref[...] * weighted[...]
+                    view[line, :] = total[:, part * LANES : (part + 1) * LANES]
+            after = []
+            for half, state, factor in zip(halves, states, scaled):
+                eighth = power_ref[2 * SUB - 2, half, cut], power_ref[2 * SUB - 1, half, cut]
+                chunk = chunk_ref[2 * j, half, cut], chunk_ref[2 * j + 1, half, cut]
+                after.append(added_product(product(factor, chunk), eighth, state))
+            return tuple(after)
+
+        lax.fori_loop(0, rows // SUB, block, start)
+    pair = 2 * SUB
     for tile in range(width // LANES):
         cut = slice(tile * LANES, (tile + 1) * LANES)
-        part = summed[:, cut]
         view = signal.at[tile]
-        for member in range(SUB):
-            part = part + view[pl.ds(member, rows, stride=SUB), :]
-        grad_key_ref[:, cut] = (part * value_ref[:, cut].astype(jnp.float32)).astype(jnp.bfloat16)
-        grad_value_ref[:, cut] = (part * key_ref[:, cut].astype(jnp.float32)).astype(jnp.bfloat16)
+        for first in range(0, rows, pair):
+            parts = []
+            for line in (first, first + SUB):
+                w = weighted[line : line + SUB, cut]
+                part = taps[0][:, cut] * w
+                for lag in range(1, SUB):
+                    part = part + taps[lag][:, cut] * pltpu.roll(w, SUB - lag, 0)
+                for member in range(SUB):
+                    part = part + view[pl.ds(line * SUB + member, SUB, stride=SUB), :]
+                parts.append(part)
+            part = jnp.concatenate(parts, axis=0)
+            both = slice(first, first + pair)
+            grad_key_ref[both, cut] = (part * value_ref[both, cut].astype(jnp.float32)).astype(jnp.bfloat16)
+            grad_value_ref[both, cut] = (part * key_ref[both, cut].astype(jnp.float32)).astype(jnp.bfloat16)
 
 
 def clip_kernel(clip_level, squares_ref, raw_ref, out_ref):
@@ -321,10 +390,16 @@
     where, grad_out = lax.optimization_barrier((lax.axis_index("seq").reshape(1), grad_out))
     scalar = [pl.BlockSpec(memory_space=pltpu.SMEM)]
     whole = pl.BlockSpec(memory_space=pltpu.VMEM)
-    packed = pl.pallas_call(
+    packed, weighted, chunks, powers, scale = pl.pallas_call(
         local_kernel,
-        out_shape=on_chip(3 * slices, LANES),
-        scratch_shapes=[pltpu.VMEM((rows, width), jnp.float32)] * 2,
+        out_shape=(
+            on_chip(3 * slices, LANES),
+            on_chip(rows, width),
+            on_chip(2 * rows // SUB, modes, width),
+            on_chip(2 * SUB, modes, width),
+            on_chip(modes, width),
+        ),
+        scratch_shapes=[pltpu.VMEM((rows, width), jnp.float32)],
         name="local_pass",
     )(grad_out, gate_query, key_input, value_input, decay_rate, pole_angle)
     own = lax.all_to_all(packed, "seq", 0, 0, tiled=True, axis_index_groups=along_z)
@@ -350,18 +425,18 @@
             on_chip(chan_shards, LANES),
         ),
         name="residue_sums",
-    )(back, decay_rate)
+    )(back)
     all_squares = kept(lax.all_to_all(squares, "chan", 0, 0, tiled=True))
     grad_key, grad_value = pl.pallas_call(
         signal_kernel,
         out_shape=(jax.ShapeDtypeStruct((rows, width), jnp.bfloat16),) * 2,
-        scratch_shapes=[
-            pltpu.VMEM((rows, width), jnp.float32),
-            pltpu.VMEM((width // LANES, rows * SUB, LANES), jnp.float32),
-        ],
+        scratch_shapes=[pltpu.VMEM((width // LANES, rows * SUB, LANES), jnp.float32)],
         cost_estimate=pl.CostEstimate(flops=20 * rows * width * modes, bytes_accessed=12 * rows * width, transcendentals=0),
         name="signal_pass",
-    )(back, grad_out, gate_query, key_input, value_input, decay_rate, pole_angle, residue, skip_gain.reshape(1, width))
+    )(
+        back, kept(weighted), kept(chunks), kept(powers), kept(scale), kept(key_input), kept(value_input),
+        kept(residue), skip_gain.reshape(1, width),
+    )
     clip_level = math.sqrt(2 * modes * width * chan_shards)
     grad_residue = pl.pallas_call(
         functools.partial(clip_kernel, clip_level),

time: 90 us -> 89 us (0.989)
  Pallas kernels: 12.1 us -> 9.97 us
  waiting for transfers between devices: 5.13 us -> 6.25 us
    pallas_call x1, Pallas kernels: 3.88 us -> 2.73 us  [on_device(): pl.pallas_call(signal_kernel, out_shape=(jax.ShapeDtypeStruct((rows, widt...]
    all_to_all x1, waiting for transfers between devices: 3.72 us -> 4.85 us  [on_device(): all_squares = kept(lax.all_to_all(squares, 'chan', 0, 0, tiled=True))]
  transfers between devices with their start and end apart: 2 -> 2, of which waited for: 2 -> 2; matrix products, arithmetic and copies ran while one was open for 0% -> 0% of each run, Pallas kernels for 4% -> 3%
where the time goes in v4:
time: 89 us; the launch traced here: 88.5 us
  blocking collectives  62.6 us (70%)
  Pallas kernels  9.97 us (11%)
  starting transfers between devices  9.01 us (10%)
  waiting for transfers between devices  6.25 us (7%)
    all_to_all x1, blocking collectives, on_device(): lax.all_to_all(packed, 'seq', 0, 0, tiled=True, axis_index_groups=along_z)  35.1 us
    all_to_all x1, blocking collectives, on_device(): lax.all_to_all(answers, 'seq', 0, 0, tiled=True, axis_index_groups=along_z)  18.8 us
    all_to_all x1, blocking collectives, on_device(): lax.all_to_all(message, 'seq', 0, 0, tiled=True, axis_index_groups=along_x)  8.71 us
    all_to_all x1, starting transfers between devices, on_device(): all_squares = kept(lax.all_to_all(squares, 'chan', 0, 0, tiled=True))  7.1 us
    all_to_all x1, waiting for transfers between devices, on_device(): all_squares = kept(lax.all_to_all(squares, 'chan', 0, 0, tiled=True))  4.85 us
    pallas_call x1, Pallas kernels, on_device(): pl.pallas_call(local_kernel, out_shape=(on_chip(3 * slices, LANES), on_ch...  3.84 us
    pallas_call x1, Pallas kernels, on_device(): pl.pallas_call(signal_kernel, out_shape=(jax.ShapeDtypeStruct((rows, widt...  2.73 us
    ppermute x1, starting transfers between devices, on_device(): lax.ppermute(own, 'seq', [(shard, shard ^ 1) for shard in range(shards)])  1.91 us
  transfers between devices with their start and end apart: 2, of which 2 were waited for; matrix products, arithmetic and copies ran while one was open for 0% of the time, Pallas kernels for 3%

profile of v4, /device:TPU:2, one launch (start us, length us, event | category | flops | bytes accessed | tf_op | source)
XLA Modules:
  0.0 88.5 jit_solution(3747318164948810067)
XLA Ops:
  0.6 3.8 %local_pass.1 = (f32[384,128]{1,0:T(8,128)S(1)}, f32[128,512]{1,0:T(8,128)S(1)}, f32[32,16,512]{2,1,0:T(8,128)S(1)}, f32[16,16,512]{2,1,0:T(8,128)S(1)}, f32[16,512]{1,0:T(8,128)S(1)}) custom-call(bf16[128,512]{1,0:T(8,128)(2,1)} %grad_ref, bf16[128,512]{1,0:T(8,128)(2,1)} %gate_ref.1, bf16[128,512]{1,0:T(8,128)(2,1)} %key_ref.3, ...), custom_call_target="tpu_custom_call" | custom-call | tf_op jit(solution)/shard_map/local_pass/pallas_call | solution.py:393
  4.5 35.1 %all_to_all.44 = f32[16,24,128]{2,1,0:T(8,128)S(1)} all-to-all(f32[16,24,128]{2,1,0:T(8,128)S(1)} %bitcast.18), channel_id=1, replica_groups={{0,16,32,48,64,80,96,112,128,144,160,176,192,208,224,240},{8,24,40,56,7..., dimensions={0} | all-to-all | bytes 393216 | tf_op jit(solution)/shard_map/all_to_all | solution.py:405
  39.6 1.9 %collective-permute-start = (f32[384,128]{1,0:T(8,128)S(1)}, f32[384,128]{1,0:T(8,128)S(1)}, u32[]{:S(2)}, u32[]{:S(2)}) collective-permute-start(f32[384,128]{1,0:T(8,128)S(1)} %bitcast.14), channel_id=1, source_target_pairs={{0,8},{8,0},{16,24},{24,16},{32,40},{40,32},{48,56},{56,48},{64,72... | collective-permute-start | bytes 589832 | tf_op jit(solution)/shard_map/ppermute | solution.py:406
  41.5 1.4 %collective-permute-done.other_ref = f32[384,128]{1,0:T(8,128)S(1)} collective-permute-done((f32[384,128]{1,0:T(8,128)S(1)}, f32[384,128]{1,0:T(8,128)S(1)}, u32[]{:S(2)}, u32[]{:S(2)}) %collective-permute-start) | collective-permute-done | bytes 196640 | tf_op jit(solution)/shard_map/ppermute | solution.py:406
  42.9 1.0 %join_run.1 = (f32[96,128]{1,0:T(8,128)S(1)}, f32[128,128]{1,0:T(8,128)S(1)}) custom-call(s32[1]{0:T(128)} %bitcast.where_ref, f32[384,128]{1,0:T(8,128)S(1)} %bitcast.15, f32[384,128]{1,0:T(8,128)S(1)} %collective-permute-done.other_ref, f32[16,512]{1,0:T(8,128)} %decay_ref.5, f32[16,512]{1,0:T(8,128)} %angle_ref.5), custom_call_target="tpu_custom_call" | custom-call | tf_op jit(solution)/shard_map/join_run/pallas_call | solution.py:407
  43.9 8.7 %all_to_all.45 = f32[4,24,128]{2,1,0:T(8,128)S(1)} all-to-all(f32[4,24,128]{2,1,0:T(8,128)S(1)} %bitcast.19), channel_id=1, replica_groups={{0,256,512,768},{8,264,520,776},{16,272,528,784},{24,280,536,792},{32,2..., dimensions={0} | all-to-all | bytes 98304 | tf_op jit(solution)/shard_map/all_to_all | solution.py:413
  52.6 0.9 %join_runs.1 = f32[256,128]{1,0:T(8,128)S(1)} custom-call(s32[1]{0:T(128)} %bitcast.where_ref, f32[96,128]{1,0:T(8,128)S(1)} %bitcast.17, f32[128,128]{1,0:T(8,128)S(1)} %get-tuple-element.20.inside_ref, f32[16,512]{1,0:T(8,128)} %decay_ref.5, f32[16,512]{1,0:T(8,128)} %angle_ref.5), custom_call_target="tpu_custom_call" | custom-call | tf_op jit(solution)/shard_map/join_runs/pallas_call | solution.py:414
  53.6 0.0 copy-start.1
  53.6 0.0 copy-start.2
  53.6 18.8 %all_to_all.46 = f32[16,16,128]{2,1,0:T(8,128)S(1)} all-to-all(f32[16,16,128]{2,1,0:T(8,128)S(1)} %bitcast.16), channel_id=1, replica_groups={{0,16,32,48,64,80,96,112,128,144,160,176,192,208,224,240},{8,24,40,56,7..., dimensions={0} | all-to-all | bytes 262144 | tf_op jit(solution)/shard_map/all_to_all | solution.py:420
  72.4 0.0 copy-start
  72.4 0.7 residue_sums.1
  73.1 7.1 %all-to-all-start.3 = ((f32[8,1,128]{2,1,0:T(1,128)}), f32[8,1,128]{2,1,0:T(1,128)S(1)}, u32[]{:S(2)}, u32[]{:S(2)}) async-start(f32[8,1,128]{2,1,0:T(1,128)} %bitcast.9), calls=%async_computation.3 | async-start | bytes 8192 | tf_op jit(solution)/shard_map/all_to_all | solution.py:429
  80.2 0.0 copy-done.1
  80.2 0.0 copy-done.2
  80.2 0.0 copy-done
  80.2 2.7 %signal_pass.1 = (bf16[128,512]{1,0:T(8,128)(2,1)}, bf16[128,512]{1,0:T(8,128)(2,1)}) custom-call(f32[256,128]{1,0:T(8,128)S(1)} %bitcast.13, f32[128,512]{1,0:T(8,128)S(1)} %get-tuple-element.21.weighted, f32[32,16,512]{2,1,0:T(8,128)S(1)} %get-tuple-element.22.chunk_ref, f32[16,16,512]{2,1,0:T(8,128)S(1)} %get-tuple-element.23.power_ref, ...), custom_call_target="tpu_custom_call" | custom-call | flops 20971520 | bytes 786432 | tf_op jit(solution)/shard_map/signal_pass/pallas_call | solution.py:430
  82.9 4.8 %all-to-all-done.3 = f32[8,1,128]{2,1,0:T(1,128)S(1)} async-done(((f32[8,1,128]{2,1,0:T(1,128)}), f32[8,1,128]{2,1,0:T(1,128)S(1)}, u32[]{:S(2)}, u32[]{:S(2)}) %all-to-all-start.3) | async-done | bytes 4128 | tf_op jit(solution)/shard_map/all_to_all | solution.py:429
  87.8 0.8 clip.1
Async XLA Ops:
  39.6 3.3 %collective-permute-start = (f32[384,128]{1,0:T(8,128)S(1)}, f32[384,128]{1,0:T(8,128)S(1)}, u32[]{:S(2)}, u32[]{:S(2)}) collective-permute-start(f32[384,128]{1,0:T(8,128)S(1)} %bitcast.14), channel_id=1, source_target_pairs={{0,8},{8,0},{16,24},{24,16},{32,40},{40,32},{48,56},{56,48},{64,72... | collective-permute-start | bytes 589832 | tf_op jit(solution)/shard_map/ppermute | solution.py:406
  53.6 26.6 %copy-start.1 = (bf16[128,512]{1,0:T(8,128)(2,1)S(1)}, bf16[128,512]{1,0:T(8,128)(2,1)}, u32[]{:S(2)}) copy-start(bf16[128,512]{1,0:T(8,128)(2,1)} %value_ref.3) | copy-start | bytes 393220
  53.6 26.6 %copy-start.2 = (f32[2,16,512]{2,1,0:T(8,128)S(1)}, f32[2,16,512]{2,1,0:T(8,128)}, u32[]{:S(2)}) copy-start(f32[2,16,512]{2,1,0:T(8,128)} %residue_ref.1) | copy-start | bytes 196612
  72.4 7.8 %copy-start = (bf16[128,512]{1,0:T(8,128)(2,1)S(1)}, bf16[128,512]{1,0:T(8,128)(2,1)}, u32[]{:S(2)}) copy-start(bf16[128,512]{1,0:T(8,128)(2,1)} %key_ref.3) | copy-start | bytes 393220
  73.1 14.7 %all-to-all-start.3 = ((f32[8,1,128]{2,1,0:T(1,128)}), f32[8,1,128]{2,1,0:T(1,128)S(1)}, u32[]{:S(2)}, u32[]{:S(2)}) async-start(f32[8,1,128]{2,1,0:T(1,128)} %bitcast.9), calls=%async_computation.3 | async-start | bytes 8192 | tf_op jit(solution)/shard_map/all_to_all | solution.py:429

commit v5 on v4

--- a/solution.py
+++ b/solution.py
@@ -6,7 +6,7 @@
 from jax import lax
 from jax.experimental import pallas as pl
 from jax.experimental.pallas import tpu as pltpu
-from jax.sharding import PartitionSpec as P
+from jax.sharding import Mesh, PartitionSpec as P
 
 LANES = 128
 HALF = 64
@@ -14,6 +14,8 @@
 CORES = 2
 CHIPS_Z = 16
 RUN = CORES * CHIPS_Z
+PART = 4
+SEQ = ("chip", "core")
 TURN_PARTS = (1.5703125, 4.837512969970703e-4, 7.54978995489188e-8)
 
 
@@ -71,12 +73,10 @@
     return jnp.concatenate(reals, axis=1), jnp.concatenate(imaginaries, axis=1)
 
 
-def answer_lines(back_ref, part, modes):
-    halves = modes // SUB
-
+def slice_lines(ref, part, parts):
     def load(block):
-        lines = [(block * halves + half) * 2 * SUB + part * SUB for half in range(halves)]
-        return jnp.concatenate([back_ref[first : first + SUB] for first in lines], axis=0)
+        lines = [((2 * block + half) * parts + part) * PART for half in range(2)]
+        return jnp.concatenate([ref[first : first + PART] for first in lines], axis=0)
 
     return load
 
@@ -93,8 +93,8 @@
 
 
 def local_kernel(
-    grad_ref, gate_ref, key_ref, value_ref, decay_ref, angle_ref,
-    packed_ref, weighted, chunk_ref, power_ref, scale_ref, stored,
+    where_ref, grad_ref, gate_ref, key_ref, value_ref, decay_ref, angle_ref,
+    keep_ref, send_ref, weighted, chunk_ref, power_ref, scale_ref, stored,
 ):
     rows = grad_ref.shape[0]
     modes, width = decay_ref.shape
@@ -131,6 +131,7 @@
         line = jnp.concatenate([totals[lag] for totals in lags], axis=1)
         line = jnp.sum(jnp.where(place < SUB - lag, line, 0.0), axis=0, keepdims=True)
         lag_sums.append(jnp.broadcast_to(line, (SUB, width)))
+    results = []
     for first in range(0, modes, SUB):
         part_rows = slice(first, first + SUB)
 
@@ -170,13 +171,37 @@
         own = scale[part_rows]
         total = total[0] * own, total[1] * own
         reach = reach[0] * own, reach[1] * own
-        for part, value in enumerate((state, total, reach)):
-
-            def store(block, value, part=part, half=first // SUB):
-                line = (block * (modes // SUB) + half) * 3 * SUB + part * SUB
-                packed_ref[line : line + SUB] = value
-
-            pack_slices(value[0], value[1], store)
+        results.append(state + total + reach)
+    first_core = core_of(where_ref) == 0
+    for part, (lower, upper) in enumerate(zip(*results)):
+        keep_ref[part] = jnp.where(first_core, lower, upper)
+        send_ref[part] = jnp.where(first_core, upper, lower)
+
+
+def shard_power(power_ref, first_core, rows):
+    real, imaginary = power_ref[2 * SUB - 2], power_ref[2 * SUB - 1]
+    power = tuple(jnp.where(first_core, part[:SUB], part[SUB:]) for part in (real, imaginary))
+    for _ in range((rows // SUB).bit_length() - 1):
+        power = product(power, power)
+    return power
+
+
+def chip_kernel(rows, where_ref, keep_ref, got_ref, power_ref, packed_ref):
+    first_core = core_of(where_ref) == 0
+    power = shard_power(power_ref, first_core, rows)
+    early = [jnp.where(first_core, keep_ref[part], got_ref[part]) for part in range(6)]
+    late = [jnp.where(first_core, got_ref[part], keep_ref[part]) for part in range(6)]
+    carry = added_product((early[0], early[1]), power, (late[0], late[1]))
+    total = added_product((early[2] + late[2], early[3] + late[3]), (early[4], early[5]), (late[0], late[1]))
+    reach = added_product((late[4], late[5]), power, (early[4], early[5]))
+    for part, value in enumerate((carry, total, reach)):
+
+        def store(block, value, part=part):
+            for half in range(2):
+                line = ((2 * block + half) * 3 + part) * PART
+                packed_ref[line : line + PART] = value[half * PART : (half + 1) * PART]
+
+        pack_slices(value[0], value[1], store)
 
 
 def swap(value):
@@ -199,93 +224,91 @@
     return direct * direct - cross * cross, 2.0 * direct * cross
 
 
-def place_of(where_ref):
-    where = where_ref[0]
-    return lax.div(where, RUN), lax.rem(lax.div(where, CORES), CHIPS_Z), lax.rem(where, CORES)
-
-
-def slice_values(ref, chip):
+def core_of(where_ref):
+    return lax.rem(where_ref[0], CORES)
+
+
+def slice_values(ref, where_ref):
     modes, width = ref.shape
-    halves = modes // SUB
-    block, half = lax.div(chip, halves), lax.rem(chip, halves)
-    chosen = jnp.zeros((SUB, LANES), jnp.float32)
+    chip, core = lax.rem(lax.div(where_ref[0], CORES), CHIPS_Z), core_of(where_ref)
+    block, half = lax.div(chip, 2), lax.rem(chip, 2)
+    chosen = jnp.zeros((PART, LANES), jnp.float32)
     for tile in range(width // LANES):
-        for first in range(halves):
-            here = (lax.div(block, 2) == tile) & (half == first)
-            part = ref[first * SUB : (first + 1) * SUB, tile * LANES : (tile + 1) * LANES]
-            chosen = jnp.where(here, part, chosen)
+        for first in range(0, modes, PART):
+            here = (lax.div(block, 2) == tile) & (core * SUB + half * PART == first)
+            chosen = jnp.where(here, ref[first : first + PART, tile * LANES : (tile + 1) * LANES], chosen)
     chosen = jnp.where(lane_low(chosen.shape) == (lax.rem(block, 2) == 0), chosen, 0.0)
     return chosen + swap(chosen)
 
 
-def span_power(span, decay_ref, angle_ref, chip):
-    decay, angle = slice_values(decay_ref, chip), slice_values(angle_ref, chip)
+def span_power(span, decay_ref, angle_ref, where_ref):
+    decay, angle = slice_values(decay_ref, where_ref), slice_values(angle_ref, where_ref)
     sine, cosine = sine_cosine(angle * float(span))
     radius = jnp.exp(-decay * float(span))
     return radius * cosine, jnp.where(lane_low(sine.shape), radius * sine, -radius * sine)
 
 
-def run_kernel(span, where_ref, own_ref, other_ref, decay_ref, angle_ref, message_ref, inside_ref):
-    _, chip, core = place_of(where_ref)
-    power = span_power(span, decay_ref, angle_ref, chip)
-    first_core = core == 0
-
-    def tiles(part, z):
-        line = (3 * z + part) * SUB
-        own, other = own_ref[line : line + SUB], other_ref[line : line + SUB]
-        pair = jnp.where(first_core, own, other), jnp.where(first_core, other, own)
-        return [(value, swap(value)) for value in pair]
-
-    zero = jnp.zeros((SUB, LANES), jnp.float32)
+def lines_of(ref, place):
+    return ref[place * PART : (place + 1) * PART]
+
+
+def run_kernel(span, where_ref, own_ref, decay_ref, angle_ref, message_ref, inside_ref, power_ref):
+    power = span_power(span, decay_ref, angle_ref, where_ref)
+    power_ref[0:PART], power_ref[PART:] = power
+    zero = jnp.zeros((PART, LANES), jnp.float32)
     state, total, reach = (zero, zero), zero, (zero, zero)
+    reaches = []
     for z in range(CHIPS_Z):
-        for value in tiles(2, z):
-            reach = step(value, reach, power)
+        value = lines_of(own_ref, 3 * z + 2)
+        reaches.append((value, swap(value)))
+        reach = step(reaches[z], reach, power)
     for z in reversed(range(CHIPS_Z)):
-        carries, sums, reaches = tiles(0, z), tiles(1, z), tiles(2, z)
-        inside = []
-        for c in reversed(range(CORES)):
-            inside.append(state[0])
-            direct, cross = factors(*reaches[c])
-            total = total + (sums[c][0] + (state[0] * direct + state[1] * cross))
-            state = step(carries[c], state, power)
-        inside_ref[z * SUB : (z + 1) * SUB] = jnp.where(first_core, inside[1], inside[0])
-    copies = message_ref.shape[0] // (3 * SUB)
-    for copy in range(copies):
+        carry = lines_of(own_ref, 3 * z)
+        inside_ref[z * PART : (z + 1) * PART] = state[0]
+        direct, cross = factors(*reaches[z])
+        total = total + (lines_of(own_ref, 3 * z + 1) + (state[0] * direct + state[1] * cross))
+        state = step((carry, swap(carry)), state, power)
+    for copy in range(message_ref.shape[0] // (3 * PART)):
         for part, value in enumerate((state[0], total, reach[0])):
-            line = (3 * copy + part) * SUB
-            message_ref[line : line + SUB] = value
-
-
-def answer_kernel(span, where_ref, message_ref, inside_ref, decay_ref, angle_ref, out_ref):
-    mine, chip, core = place_of(where_ref)
-    power = span_power(span, decay_ref, angle_ref, chip)
+            line = (3 * copy + part) * PART
+            message_ref[line : line + PART] = value
+
+
+def answer_kernel(where_ref, message_ref, inside_ref, power_ref, out_ref):
+    mine = lax.div(where_ref[0], RUN)
+    power = power_ref[0:PART], power_ref[PART:]
     run_power = power
-    for _ in range(RUN.bit_length() - 1):
+    for _ in range(CHIPS_Z.bit_length() - 1):
         run_power = squared(run_power)
-    zero = jnp.zeros((SUB, LANES), jnp.float32)
+    zero = jnp.zeros((PART, LANES), jnp.float32)
     state, total = (zero, zero), zero
     entering = (zero, zero)
-    for x in reversed(range(message_ref.shape[0] // (3 * SUB))):
-        carry, sums, reach = [message_ref[(3 * x + part) * SUB : (3 * x + part + 1) * SUB] for part in range(3)]
+    for x in reversed(range(message_ref.shape[0] // (3 * PART))):
+        carry, sums, reach = [lines_of(message_ref, 3 * x + part) for part in range(3)]
         entering = tuple(jnp.where(mine == x, new, old) for new, old in zip(state, entering))
         direct, cross = factors(reach, swap(reach))
         total = total + (sums + (state[0] * direct + state[1] * cross))
         state = step((carry, swap(carry)), state, run_power)
-    moved = step((zero, zero), entering, power)
-    entering = tuple(jnp.where(core == CORES - 1, here, there) for here, there in zip(entering, moved))
-    chip_power = squared(power)
     for z in reversed(range(CHIPS_Z)):
-        out_ref[2 * z * SUB : (2 * z + 1) * SUB] = inside_ref[z * SUB : (z + 1) * SUB] + entering[0]
-        out_ref[(2 * z + 1) * SUB : (2 * z + 2) * SUB] = total
-        entering = step((zero, zero), entering, chip_power)
-
-
-def residue_kernel(back_ref, raw_ref, squares_ref):
-    _, modes, width = raw_ref.shape
-    real, imaginary = unpack_slices(answer_lines(back_ref, 1, modes), modes, width)
-    raw_ref[0] = real
-    raw_ref[1] = -imaginary
+        out_ref[2 * z * PART : (2 * z + 1) * PART] = lines_of(inside_ref, z) + entering[0]
+        out_ref[(2 * z + 1) * PART : (2 * z + 2) * PART] = total
+        entering = step((zero, zero), entering, power)
+
+
+def residue_kernel(rows, where_ref, back_ref, keep_ref, got_ref, power_ref, mine_ref, send_ref, squares_ref):
+    _, modes, width = mine_ref.shape
+    first_core = core_of(where_ref) == 0
+    power = shard_power(power_ref, first_core, rows)
+    late = unpack_slices(slice_lines(back_ref, 0, 2), modes, width)
+    carry = tuple(jnp.where(first_core, got_ref[part], keep_ref[part]) for part in range(2))
+    early = added_product(carry, power, late)
+    real, imaginary = unpack_slices(slice_lines(back_ref, 1, 2), modes, width)
+    for part in range(2):
+        mine_ref[part] = jnp.where(first_core, early[part], late[part])
+        send_ref[part] = jnp.where(first_core, late[part], early[part])
+    for ref in (mine_ref, send_ref):
+        ref[2] = real
+        ref[3] = -imaginary
     squares = jnp.sum(real * real + imaginary * imaginary, axis=0, keepdims=True)
     total = squares[:, 0:LANES]
     for tile in range(1, width // LANES):
@@ -293,8 +316,14 @@
     squares_ref[...] = jnp.broadcast_to(total, squares_ref.shape)
 
 
+def both_halves(where_ref, mine_ref, other_ref, part):
+    first_core = core_of(where_ref) == 0
+    mine, other = mine_ref[part], other_ref[part]
+    return jnp.concatenate([jnp.where(first_core, mine, other), jnp.where(first_core, other, mine)], axis=0)
+
+
 def signal_kernel(
-    back_ref, weighted, chunk_ref, power_ref, scale_ref, key_ref, value_ref, residue_ref, skip_ref,
+    where_ref, mine_ref, other_ref, weighted, chunk_ref, power_ref, scale_ref, key_ref, value_ref, residue_ref, skip_ref,
     grad_key_ref, grad_value_ref, signal,
 ):
     rows, width = weighted.shape
@@ -311,7 +340,7 @@
         line = jnp.broadcast_to(jnp.sum(tap, axis=0, keepdims=True), (SUB, width))
         taps.append(jnp.where(place < SUB - lag, line, 0.0))
     taps[0] = taps[0] + skip_ref[...]
-    begin = product(weight, unpack_slices(answer_lines(back_ref, 0, modes), modes, width))
+    begin = product(weight, tuple(both_halves(where_ref, mine_ref, other_ref, part) for part in range(2)))
     span = 2 * LANES
     for column in range(0, width, span):
         cut = slice(column, column + span)
@@ -359,9 +388,12 @@
             grad_value_ref[both, cut] = (part * key_ref[both, cut].astype(jnp.float32)).astype(jnp.bfloat16)
 
 
-def clip_kernel(clip_level, squares_ref, raw_ref, out_ref):
+def clip_kernel(clip_level, where_ref, squares_ref, mine_ref, other_ref, after_ref, out_ref):
+    del after_ref
     norm = jnp.sqrt(jnp.sum(squares_ref[...], keepdims=True))
-    out_ref[...] = raw_ref[...] * (clip_level / jnp.maximum(norm, clip_level))[None]
+    factor = clip_level / jnp.maximum(norm, clip_level)
+    for part in range(2):
+        out_ref[part] = both_halves(where_ref, mine_ref, other_ref, 2 + part) * factor
 
 
 def on_chip(*shape):
@@ -384,16 +416,19 @@
 ):
     rows, width = grad_out.shape
     modes = decay_rate.shape[0]
-    shards, chan_shards = lax.axis_size("seq"), lax.axis_size("chan")
-    slices = modes * width // HALF
+    shards, chan_shards = lax.axis_size(SEQ), lax.axis_size("chan")
+    runs = shards // RUN
     along_z, along_x = groups(shards)
-    where, grad_out = lax.optimization_barrier((lax.axis_index("seq").reshape(1), grad_out))
-    scalar = [pl.BlockSpec(memory_space=pltpu.SMEM)]
+    flip = [(shard, shard ^ 1) for shard in range(shards)]
+    where, grad_out = lax.optimization_barrier((lax.axis_index(SEQ).reshape(1), grad_out))
+    scalar = pl.BlockSpec(memory_space=pltpu.SMEM)
     whole = pl.BlockSpec(memory_space=pltpu.VMEM)
-    packed, weighted, chunks, powers, scale = pl.pallas_call(
+    keep, send, weighted, chunks, powers, scale = pl.pallas_call(
         local_kernel,
+        in_specs=[scalar] + [whole] * 6,
         out_shape=(
-            on_chip(3 * slices, LANES),
+            on_chip(6, SUB, width),
+            on_chip(6, SUB, width),
             on_chip(rows, width),
             on_chip(2 * rows // SUB, modes, width),
             on_chip(2 * SUB, modes, width),
@@ -401,65 +436,85 @@
         ),
         scratch_shapes=[pltpu.VMEM((rows, width), jnp.float32)],
         name="local_pass",
-    )(grad_out, gate_query, key_input, value_input, decay_rate, pole_angle)
-    own = lax.all_to_all(packed, "seq", 0, 0, tiled=True, axis_index_groups=along_z)
-    other = lax.ppermute(own, "seq", [(shard, shard ^ 1) for shard in range(shards)])
-    message, inside = pl.pallas_call(
-        functools.partial(run_kernel, rows),
-        in_specs=scalar + [whole] * 4,
-        out_shape=(on_chip(3 * SUB * (shards // RUN), LANES), on_chip(CHIPS_Z * SUB, LANES)),
+    )(where, grad_out, gate_query, key_input, value_input, decay_rate, pole_angle)
+    keep, powers = kept(keep), kept(powers)
+    got = kept(lax.ppermute(send, SEQ, flip))
+    packed = pl.pallas_call(
+        functools.partial(chip_kernel, rows),
+        in_specs=[scalar] + [whole] * 3,
+        out_shape=on_chip(3 * CHIPS_Z * PART, LANES),
+        name="join_chip",
+    )(where, keep, got, powers)
+    own = kept(exchange(packed, CHIPS_Z, along_z))
+    message, inside, power = pl.pallas_call(
+        functools.partial(run_kernel, CORES * rows),
+        in_specs=[scalar] + [whole] * 3,
+        out_shape=(on_chip(3 * PART * runs, LANES), on_chip(CHIPS_Z * PART, LANES), on_chip(2 * PART, LANES)),
         name="join_run",
-    )(where, kept(own), kept(other), decay_rate, pole_angle)
-    message = lax.all_to_all(message, "seq", 0, 0, tiled=True, axis_index_groups=along_x)
+    )(where, own, kept(decay_rate), kept(pole_angle))
+    message = kept(exchange(message, runs, along_x))
     answers = pl.pallas_call(
-        functools.partial(answer_kernel, rows),
-        in_specs=scalar + [whole] * 4,
-        out_shape=on_chip(2 * CHIPS_Z * SUB, LANES),
+        answer_kernel,
+        in_specs=[scalar] + [whole] * 3,
+        out_shape=on_chip(2 * CHIPS_Z * PART, LANES),
         name="join_runs",
-    )(where, kept(message), kept(inside), decay_rate, pole_angle)
-    back = kept(lax.all_to_all(answers, "seq", 0, 0, tiled=True, axis_index_groups=along_z))
-    raw, squares = pl.pallas_call(
-        residue_kernel,
+    )(where, message, kept(inside), kept(power))
+    back = kept(exchange(answers, CHIPS_Z, along_z))
+    mine, send, squares = pl.pallas_call(
+        functools.partial(residue_kernel, rows),
+        in_specs=[scalar] + [whole] * 4,
         out_shape=(
-            on_chip(2, modes, width),
-            on_chip(chan_shards, LANES),
+            on_chip(4, SUB, width),
+            on_chip(4, SUB, width),
+            on_chip(CORES * chan_shards, LANES),
         ),
         name="residue_sums",
-    )(back)
-    all_squares = kept(lax.all_to_all(squares, "chan", 0, 0, tiled=True))
+    )(where, back, keep, got, powers)
+    other = kept(lax.ppermute(send, SEQ, flip))
+    mine = kept(mine)
+    all_squares = kept(lax.all_to_all(squares, ("core", "chan"), 0, 0, tiled=True))
     grad_key, grad_value = pl.pallas_call(
         signal_kernel,
+        in_specs=[scalar] + [whole] * 10,
         out_shape=(jax.ShapeDtypeStruct((rows, width), jnp.bfloat16),) * 2,
         scratch_shapes=[pltpu.VMEM((width // LANES, rows * SUB, LANES), jnp.float32)],
         cost_estimate=pl.CostEstimate(flops=20 * rows * width * modes, bytes_accessed=12 * rows * width, transcendentals=0),
         name="signal_pass",
     )(
-        back, kept(weighted), kept(chunks), kept(powers), kept(scale), kept(key_input), kept(value_input),
+        where, mine, other, kept(weighted), kept(chunks), powers, kept(scale), kept(key_input), kept(value_input),
         kept(residue), skip_gain.reshape(1, width),
     )
     clip_level = math.sqrt(2 * modes * width * chan_shards)
     grad_residue = pl.pallas_call(
         functools.partial(clip_kernel, clip_level),
+        in_specs=[scalar] + [whole] * 3 + [pl.BlockSpec(memory_space=pl.ANY)],
         out_shape=jax.ShapeDtypeStruct((2, modes, width), jnp.float32),
         name="clip",
-    )(all_squares, kept(raw))
+    )(where, all_squares, mine, other, grad_key)
     return (grad_key, grad_value, grad_residue)
 
 
+def exchange(array, members, over):
+    sent = array.reshape(members, -1)
+    return lax.all_to_all(sent, SEQ, 0, 0, tiled=True, axis_index_groups=over).reshape(array.shape)
+
+
 def solution(mesh):
+    shards, chan_shards = mesh.devices.shape
+    split = Mesh(mesh.devices.reshape(shards // CORES, CORES, chan_shards), ("chip", "core", "chan"))
     return jax.shard_map(
         on_device,
-        mesh=mesh,
+        mesh=split,
         in_specs=(
-            P("seq", "chan"),
-            P("seq", "chan"),
-            P("seq", "chan"),
-            P("seq", "chan"),
+            P(SEQ, "chan"),
+            P(SEQ, "chan"),
+            P(SEQ, "chan"),
+            P(SEQ, "chan"),
             P(None, "chan"),
             P(None, "chan"),
             P(None, None, "chan"),
             P("chan"),
         ),
-        out_specs=(P("seq", "chan"), P("seq", "chan"), P(None, None, "chan")),
+        out_specs=(P(SEQ, "chan"), P(SEQ, "chan"), P(None, None, "chan")),
         check_vma=False,
     )

time: 89 us -> 85.4 us (0.960)
  the two profiles are of different devices: /device:TPU:2 before, /device:TPU:1 now
where the time goes in v5:
time: 85.4 us; the launch traced here: 85 us
  blocking collectives  42.1 us (49%)
  starting transfers between devices  28.8 us (34%)
  Pallas kernels  8.32 us (10%)
  waiting for transfers between devices  5.07 us (6%)
    all_to_all x3, blocking collectives, exchange(): lax.all_to_all(sent, SEQ, 0, 0, tiled=True, axis_index_groups=over)  42.1 us
    ppermute x1, starting transfers between devices, on_device(): got = kept(lax.ppermute(send, SEQ, flip))  16.1 us
    all_to_all x1, starting transfers between devices, on_device(): lax.all_to_all(squares, ('core', 'chan'), 0, 0, tiled=True)  7.24 us
    ppermute x1, starting transfers between devices, on_device(): other = kept(lax.ppermute(send, SEQ, flip))  5.46 us
    all_to_all x1, waiting for transfers between devices, on_device(): lax.all_to_all(squares, ('core', 'chan'), 0, 0, tiled=True)  4.14 us
    pallas_call x1, Pallas kernels, on_device(): pl.pallas_call(local_kernel, in_specs=[scalar] + [whole] * 6, out_shape=(...  3.74 us
    pallas_call x1, Pallas kernels, on_device(): pl.pallas_call(signal_kernel, in_specs=[scalar] + [whole] * 10, out_shape...  2.71 us
  transfers between devices with their start and end apart: 3, of which 2 were waited for; matrix products, arithmetic and copies ran while one was open for 0% of the time, Pallas kernels for 3%

profile of v5, /device:TPU:1, one launch (start us, length us, event | category | flops | bytes accessed | tf_op | source)
XLA Modules:
  0.0 85.0 jit_solution(6051260940606956143)
XLA Ops:
  0.6 3.7 %local_pass.1 = (f32[6,8,512]{2,1,0:T(8,128)S(1)}, f32[6,8,512]{2,1,0:T(8,128)S(1)}, f32[128,512]{1,0:T(8,128)S(1)}, f32[32,16,512]{2,1,0:T(8,128)S(1)}, f32[16,...) custom-call(s32[1]{0:T(128)} %bitcast.where_ref, bf16[128,512]{1,0:T(8,128)(2,1)} %grad_ref, bf16[128,512]{1,0:T(8,128)(2,1)} %gate_ref.1, ...), custom_call_target="tpu_custom_call" | custom-call | tf_op jit(solution)/shard_map/local_pass/pallas_call | solution.py:426
  4.4 16.1 %collective-permute-start = (f32[6,8,512]{2,1,0:T(8,128)S(1)}, f32[6,8,512]{2,1,0:T(8,128)S(1)}, u32[]{:S(2)}, u32[]{:S(2)}) collective-permute-start(f32[6,8,512]{2,1,0:T(8,128)S(1)} %get-tuple-element.22), channel_id=1, source_target_pairs={{0,8},{8,0},{16,24},{24,16},{32,40},{40,32},{48,56},{56,48},{64,72... | collective-permute-start | bytes 294920 | tf_op jit(solution)/shard_map/ppermute | solution.py:441
  20.5 0.9 %collective-permute-done.got_ref = f32[6,8,512]{2,1,0:T(8,128)S(1)} collective-permute-done((f32[6,8,512]{2,1,0:T(8,128)S(1)}, f32[6,8,512]{2,1,0:T(8,128)S(1)}, u32[]{:S(2)}, u32[]{:S(2)}) %collective-permute-start) | collective-permute-done | bytes 98336 | tf_op jit(solution)/shard_map/ppermute | solution.py:441
  21.4 0.1 join_chip.1
  21.5 0.0 copy-start.2
  21.5 0.0 copy-start.3
  21.5 17.6 %all_to_all.38 = f32[16,1,1536]{2,1,0:T(1,128)S(1)} all-to-all(f32[16,1,1536]{2,1,0:T(1,128)S(1)} %bitcast.13), channel_id=1, replica_groups={{0,16,32,48,64,80,96,112,128,144,160,176,192,208,224,240},{8,24,40,56,7..., dimensions={0} | all-to-all | bytes 196608 | tf_op jit(solution)/shard_map/all_to_all | solution.py:499
  39.1 0.0 copy-done.2
  39.2 0.0 copy-done.3
  39.2 0.2 join_run.1
  39.3 8.1 %all_to_all.39 = f32[4,1,1536]{2,1,0:T(1,128)S(1)} all-to-all(f32[4,1,1536]{2,1,0:T(1,128)S(1)} %bitcast.18), channel_id=1, replica_groups={{0,256,512,768},{8,264,520,776},{16,272,528,784},{24,280,536,792},{32,2..., dimensions={0} | all-to-all | bytes 49152 | tf_op jit(solution)/shard_map/all_to_all | solution.py:499
  47.4 0.1 join_runs.1
  47.5 16.4 %all_to_all.40 = f32[16,1,1024]{2,1,0:T(1,128)S(1)} all-to-all(f32[16,1,1024]{2,1,0:T(1,128)S(1)} %bitcast.14), channel_id=1, replica_groups={{0,16,32,48,64,80,96,112,128,144,160,176,192,208,224,240},{8,24,40,56,7..., dimensions={0} | all-to-all | bytes 131072 | tf_op jit(solution)/shard_map/all_to_all | solution.py:499
  63.9 0.0 copy-start
  63.9 0.7 residue_sums.1
  64.6 5.5 %collective-permute-start.1 = (f32[4,8,512]{2,1,0:T(8,128)S(1)}, f32[4,8,512]{2,1,0:T(8,128)S(1)}, u32[]{:S(2)}, u32[]{:S(2)}) collective-permute-start(f32[4,8,512]{2,1,0:T(8,128)S(1)} %get-tuple-element.28), channel_id=1, source_target_pairs={{0,8},{8,0},{16,24},{24,16},{32,40},{40,32},{48,56},{56,48},{64,72... | collective-permute-start | bytes 196616 | tf_op jit(solution)/shard_map/ppermute | solution.py:473
  70.1 7.2 %all-to-all-start.3 = ((f32[16,1,128]{2,1,0:T(1,128)}), f32[16,1,128]{2,1,0:T(1,128)S(1)}, u32[]{:S(2)}, u32[]{:S(2)}) async-start(f32[16,1,128]{2,1,0:T(1,128)} %bitcast.9), calls=%async_computation.3 | async-start | bytes 16384 | tf_op jit(solution)/shard_map/all_to_all | solution.py:475
  77.3 0.0 collective-permute-done.1.other_ref
  77.3 0.0 copy-done
  77.3 0.0 copy-done.1
  77.3 0.0 copy-done.4
  77.4 2.7 %signal_pass.1 = (bf16[128,512]{1,0:T(8,128)(2,1)}, bf16[128,512]{1,0:T(8,128)(2,1)}) custom-call(s32[1]{0:T(128)} %bitcast.where_ref, f32[4,8,512]{2,1,0:T(8,128)S(1)} %get-tuple-element.27.mine_ref, f32[4,8,512]{2,1,0:T(8,128)S(1)} %collective-permute-done.1.other_ref, f32[128,512]{1,0:T(8,128)S(1)} %get-tuple-element.29.weighted, ...), custom_call_target="tpu_custom_call" | custom-call | flops 20971520 | bytes 786432 | tf_op jit(solution)/shard_map/signal_pass/pallas_call | solution.py:476
  80.1 4.1 %all-to-all-done.3 = f32[16,1,128]{2,1,0:T(1,128)S(1)} async-done(((f32[16,1,128]{2,1,0:T(1,128)}), f32[16,1,128]{2,1,0:T(1,128)S(1)}, u32[]{:S(2)}, u32[]{:S(2)}) %all-to-all-start.3) | async-done | bytes 8224 | tf_op jit(solution)/shard_map/all_to_all | solution.py:475
  84.2 0.8 clip.1
  (2 shorter events, 0.0 us)
Async XLA Ops:
  4.4 17.0 %collective-permute-start = (f32[6,8,512]{2,1,0:T(8,128)S(1)}, f32[6,8,512]{2,1,0:T(8,128)S(1)}, u32[]{:S(2)}, u32[]{:S(2)}) collective-permute-start(f32[6,8,512]{2,1,0:T(8,128)S(1)} %get-tuple-element.22), channel_id=1, source_target_pairs={{0,8},{8,0},{16,24},{24,16},{32,40},{40,32},{48,56},{56,48},{64,72... | collective-permute-start | bytes 294920 | tf_op jit(solution)/shard_map/ppermute | solution.py:441
  21.5 17.7 %copy-start.2 = (f32[16,512]{1,0:T(8,128)S(1)}, f32[16,512]{1,0:T(8,128)}, u32[]{:S(2)}) copy-start(f32[16,512]{1,0:T(8,128)} %decay_ref.3) | copy-start | bytes 98308
  21.5 17.7 %copy-start.3 = (f32[16,512]{1,0:T(8,128)S(1)}, f32[16,512]{1,0:T(8,128)}, u32[]{:S(2)}) copy-start(f32[16,512]{1,0:T(8,128)} %angle_ref.3) | copy-start | bytes 98308
  63.9 13.4 %copy-start = (bf16[128,512]{1,0:T(8,128)(2,1)S(1)}, bf16[128,512]{1,0:T(8,128)(2,1)}, u32[]{:S(2)}) copy-start(bf16[128,512]{1,0:T(8,128)(2,1)} %key_ref.3) | copy-start | bytes 393220
  63.9 13.4 %copy-start.1 = (bf16[128,512]{1,0:T(8,128)(2,1)S(1)}, bf16[128,512]{1,0:T(8,128)(2,1)}, u32[]{:S(2)}) copy-start(bf16[128,512]{1,0:T(8,128)(2,1)} %value_ref.3) | copy-start | bytes 393220
  63.9 13.4 %copy-start.4 = (f32[2,16,512]{2,1,0:T(8,128)S(1)}, f32[2,16,512]{2,1,0:T(8,128)}, u32[]{:S(2)}) copy-start(f32[2,16,512]{2,1,0:T(8,128)} %residue_ref.1) | copy-start | bytes 196612
  64.6 12.7 %collective-permute-start.1 = (f32[4,8,512]{2,1,0:T(8,128)S(1)}, f32[4,8,512]{2,1,0:T(8,128)S(1)}, u32[]{:S(2)}, u32[]{:S(2)}) collective-permute-start(f32[4,8,512]{2,1,0:T(8,128)S(1)} %get-tuple-element.28), channel_id=1, source_target_pairs={{0,8},{8,0},{16,24},{24,16},{32,40},{40,32},{48,56},{56,48},{64,72... | collective-permute-start | bytes 196616 | tf_op jit(solution)/shard_map/ppermute | solution.py:473
  70.1 14.1 %all-to-all-start.3 = ((f32[16,1,128]{2,1,0:T(1,128)}), f32[16,1,128]{2,1,0:T(1,128)S(1)}, u32[]{:S(2)}, u32[]{:S(2)}) async-start(f32[16,1,128]{2,1,0:T(1,128)} %bitcast.9), calls=%async_computation.3 | async-start | bytes 16384 | tf_op jit(solution)/shard_map/all_to_all | solution.py:475

commit v6 on v5

--- a/solution.py
+++ b/solution.py
@@ -92,26 +92,73 @@
     )
 
 
-def local_kernel(
+def chosen_half(first, array):
+    half = array.shape[0] // 2
+    return jnp.where(first, array[:half], array[half:])
+
+
+def half_pass(weighted, stored, lag_sums, base, scale, result_ref, chunk_ref, power_ref):
+    rows, width = weighted.shape
+    powers = [base]
+    for k in range(2, SUB + 1):
+        powers.append(product(powers[k // 2 - 1], powers[k - k // 2 - 1]))
+    for k in range(SUB):
+        power_ref[2 * k], power_ref[2 * k + 1] = powers[k]
+
+    def power(k):
+        return power_ref[2 * k - 2], power_ref[2 * k - 1]
+
+    def block(i, carry):
+        state, total, reach, far = carry
+        j = rows // SUB - 1 - i
+        ws, ss = line_block(weighted, j * SUB), line_block(stored, j * SUB)
+        eighth = power(SUB)
+        chunk_real, chunk_imaginary = ws[0], None
+        answer_real, answer_imaginary = ss[0] * eighth[0], ss[0] * eighth[1]
+        for k in range(1, SUB):
+            real, imaginary = power(k)
+            chunk_real = chunk_real + ws[k] * real
+            cross = ws[k] * imaginary
+            chunk_imaginary = cross if chunk_imaginary is None else chunk_imaginary + cross
+            answer_real = answer_real + ss[SUB - k] * real
+            answer_imaginary = answer_imaginary + ss[SUB - k] * imaginary
+        chunk, answer = (chunk_real, chunk_imaginary), (answer_real, answer_imaginary)
+        chunk_ref[2 * j] = chunk_real
+        chunk_ref[2 * j + 1] = chunk_imaginary
+        total = added_product(total, answer, state)
+        reach = added_product(reach, answer, far)
+        return added_product(chunk, eighth, state), total, reach, product(far, eighth)
+
+    zero = jnp.zeros((SUB, width), jnp.float32)
+    pair = (zero, zero)
+    state, total, reach, _ = lax.fori_loop(
+        0, rows // SUB, block, (pair, pair, pair, (jnp.ones((SUB, width), jnp.float32), zero))
+    )
+    total = total[0] + lag_sums[0], total[1]
+    for lag in range(1, SUB):
+        real, imaginary = power(lag)
+        total = total[0] + lag_sums[lag] * real, total[1] + lag_sums[lag] * imaginary
+    result_ref[0], result_ref[1] = state
+    for part in range(2):
+        result_ref[2 + part] = total[part] * scale
+        result_ref[4 + part] = reach[part] * scale
+
+
+def first_kernel(
     where_ref, grad_ref, gate_ref, key_ref, value_ref, decay_ref, angle_ref,
-    keep_ref, send_ref, weighted, chunk_ref, power_ref, scale_ref, stored,
+    send_ref, chunk_ref, power_ref, weighted, stored, lag_ref, base_ref, scale_ref,
 ):
-    rows = grad_ref.shape[0]
-    modes, width = decay_ref.shape
+    rows, width = grad_ref.shape
     weighted[...] = grad_ref[...].astype(jnp.float32) * gate_ref[...].astype(jnp.float32)
     stored[...] = key_ref[...].astype(jnp.float32) * value_ref[...].astype(jnp.float32)
     decay = decay_ref[...]
     sine, cosine = sine_cosine(angle_ref[...])
     radius = jnp.exp(-decay)
     base = (radius * cosine, -radius * sine)
-    powers = [base]
-    for k in range(2, SUB + 1):
-        powers.append(product(powers[k // 2 - 1], powers[k - k // 2 - 1]))
-    for k in range(SUB):
-        power_ref[2 * k] = powers[k][0]
-        power_ref[2 * k + 1] = powers[k][1]
     scale = scale_of(decay)
-    scale_ref[...] = scale
+    first_core = core_of(where_ref) == 0
+    base_ref[0], base_ref[1] = [chosen_half(first_core, part) for part in base]
+    scale_ref[...] = chosen_half(first_core, scale)
     lags = []
     for tile in range(width // LANES):
         cut = slice(tile * LANES, (tile + 1) * LANES)
@@ -131,56 +178,23 @@
         line = jnp.concatenate([totals[lag] for totals in lags], axis=1)
         line = jnp.sum(jnp.where(place < SUB - lag, line, 0.0), axis=0, keepdims=True)
         lag_sums.append(jnp.broadcast_to(line, (SUB, width)))
-    results = []
-    for first in range(0, modes, SUB):
-        part_rows = slice(first, first + SUB)
-
-        def power(k, part_rows=part_rows):
-            return power_ref[2 * k - 2, part_rows], power_ref[2 * k - 1, part_rows]
-
-        def block(i, carry, power=power, part_rows=part_rows):
-            state, total, reach, far = carry
-            j = rows // SUB - 1 - i
-            ws, ss = line_block(weighted, j * SUB), line_block(stored, j * SUB)
-            eighth = power(SUB)
-            chunk_real, chunk_imaginary = ws[0], None
-            answer_real, answer_imaginary = ss[0] * eighth[0], ss[0] * eighth[1]
-            for k in range(1, SUB):
-                real, imaginary = power(k)
-                chunk_real = chunk_real + ws[k] * real
-                cross = ws[k] * imaginary
-                chunk_imaginary = cross if chunk_imaginary is None else chunk_imaginary + cross
-                answer_real = answer_real + ss[SUB - k] * real
-                answer_imaginary = answer_imaginary + ss[SUB - k] * imaginary
-            chunk, answer = (chunk_real, chunk_imaginary), (answer_real, answer_imaginary)
-            chunk_ref[2 * j, part_rows] = chunk_real
-            chunk_ref[2 * j + 1, part_rows] = chunk_imaginary
-            total = added_product(total, answer, state)
-            reach = added_product(reach, answer, far)
-            return added_product(chunk, eighth, state), total, reach, product(far, eighth)
-
-        zero = jnp.zeros((SUB, width), jnp.float32)
-        pair = (zero, zero)
-        state, total, reach, _ = lax.fori_loop(
-            0, rows // SUB, block, (pair, pair, pair, (jnp.ones((SUB, width), jnp.float32), zero))
-        )
-        total = total[0] + lag_sums[0], total[1]
-        for lag in range(1, SUB):
-            real, imaginary = power(lag)
-            total = total[0] + lag_sums[lag] * real, total[1] + lag_sums[lag] * imaginary
-        own = scale[part_rows]
-        total = total[0] * own, total[1] * own
-        reach = reach[0] * own, reach[1] * own
-        results.append(state + total + reach)
-    first_core = core_of(where_ref) == 0
-    for part, (lower, upper) in enumerate(zip(*results)):
-        keep_ref[part] = jnp.where(first_core, lower, upper)
-        send_ref[part] = jnp.where(first_core, upper, lower)
-
-
-def shard_power(power_ref, first_core, rows):
-    real, imaginary = power_ref[2 * SUB - 2], power_ref[2 * SUB - 1]
-    power = tuple(jnp.where(first_core, part[:SUB], part[SUB:]) for part in (real, imaginary))
+        lag_ref[lag] = lag_sums[lag]
+    other = core_of(where_ref) != 0
+    half_pass(
+        weighted, stored, lag_sums, tuple(chosen_half(other, part) for part in base), chosen_half(other, scale),
+        send_ref, chunk_ref, power_ref,
+    )
+
+
+def second_kernel(weighted, stored, lag_ref, base_ref, scale_ref, keep_ref, chunk_ref, power_ref):
+    lag_sums = [lag_ref[lag] for lag in range(SUB)]
+    half_pass(
+        weighted, stored, lag_sums, (base_ref[0], base_ref[1]), scale_ref[...], keep_ref, chunk_ref, power_ref
+    )
+
+
+def shard_power(power_ref, rows):
+    power = power_ref[2 * SUB - 2], power_ref[2 * SUB - 1]
     for _ in range((rows // SUB).bit_length() - 1):
         power = product(power, power)
     return power
@@ -188,7 +202,7 @@
 
 def chip_kernel(rows, where_ref, keep_ref, got_ref, power_ref, packed_ref):
     first_core = core_of(where_ref) == 0
-    power = shard_power(power_ref, first_core, rows)
+    power = shard_power(power_ref, rows)
     early = [jnp.where(first_core, keep_ref[part], got_ref[part]) for part in range(6)]
     late = [jnp.where(first_core, got_ref[part], keep_ref[part]) for part in range(6)]
     carry = added_product((early[0], early[1]), power, (late[0], late[1]))
@@ -298,7 +312,7 @@
 def residue_kernel(rows, where_ref, back_ref, keep_ref, got_ref, power_ref, mine_ref, send_ref, squares_ref):
     _, modes, width = mine_ref.shape
     first_core = core_of(where_ref) == 0
-    power = shard_power(power_ref, first_core, rows)
+    power = shard_power(power_ref, rows)
     late = unpack_slices(slice_lines(back_ref, 0, 2), modes, width)
     carry = tuple(jnp.where(first_core, got_ref[part], keep_ref[part]) for part in range(2))
     early = added_product(carry, power, late)
@@ -323,47 +337,48 @@
 
 
 def signal_kernel(
-    where_ref, mine_ref, other_ref, weighted, chunk_ref, power_ref, scale_ref, key_ref, value_ref, residue_ref, skip_ref,
-    grad_key_ref, grad_value_ref, signal,
+    where_ref, mine_ref, other_ref, weighted, my_chunks, other_chunks, my_powers, other_powers, decay_ref, key_ref,
+    value_ref, residue_ref, skip_ref, grad_key_ref, grad_value_ref, signal,
 ):
     rows, width = weighted.shape
-    modes = scale_ref.shape[0]
-    scale = scale_ref[...]
+    scale = scale_of(decay_ref[...])
+    first_core = core_of(where_ref) == 0
     weight = residue_ref[0] * scale, residue_ref[1] * scale
+    chunk_refs, power_refs = (my_chunks, other_chunks), (my_powers, other_powers)
+    weights = [tuple(chosen_half(first, part) for part in weight) for first in (first_core, core_of(where_ref) != 0)]
     place = lax.broadcasted_iota(jnp.int32, (SUB, width), 0)
     taps = []
     for lag in range(SUB):
-        if lag:
-            tap = weight[0] * power_ref[2 * lag - 2] - weight[1] * power_ref[2 * lag - 1]
-        else:
-            tap = weight[0]
+        tap = None
+        for half, powers in zip(weights, power_refs):
+            part = half[0] * powers[2 * lag - 2] - half[1] * powers[2 * lag - 1] if lag else half[0]
+            tap = part if tap is None else tap + part
         line = jnp.broadcast_to(jnp.sum(tap, axis=0, keepdims=True), (SUB, width))
         taps.append(jnp.where(place < SUB - lag, line, 0.0))
     taps[0] = taps[0] + skip_ref[...]
-    begin = product(weight, tuple(both_halves(where_ref, mine_ref, other_ref, part) for part in range(2)))
+    begins = [product(half, (states[0], states[1])) for half, states in zip(weights, (mine_ref, other_ref))]
     span = 2 * LANES
     for column in range(0, width, span):
         cut = slice(column, column + span)
-        halves = [slice(first, first + SUB) for first in range(0, modes, SUB)]
-        scaled = [tuple(part[half, cut] for part in weight) for half in halves]
-        start = tuple(tuple(part[half, cut] for part in begin) for half in halves)
-
-        def block(i, states, cut=cut, halves=halves, scaled=scaled):
+        scaled = [tuple(part[:, cut] for part in half) for half in weights]
+        start = tuple(tuple(part[:, cut] for part in begin) for begin in begins)
+
+        def block(i, states, cut=cut, scaled=scaled):
             j = rows // SUB - 1 - i
             for r in range(SUB):
                 k = SUB - r
                 total = None
-                for half, state in zip(halves, states):
-                    part = power_ref[2 * k - 2, half, cut] * state[0] - power_ref[2 * k - 1, half, cut] * state[1]
+                for powers, state in zip(power_refs, states):
+                    part = powers[2 * k - 2, :, cut] * state[0] - powers[2 * k - 1, :, cut] * state[1]
                     total = part if total is None else total + part
                 line = pl.ds(pl.multiple_of((j * SUB + r) * SUB, SUB), SUB)
                 for part in range(span // LANES):
                     view = signal.at[cut.start // LANES + part]
                     view[line, :] = total[:, part * LANES : (part + 1) * LANES]
             after = []
-            for half, state, factor in zip(halves, states, scaled):
-                eighth = power_ref[2 * SUB - 2, half, cut], power_ref[2 * SUB - 1, half, cut]
-                chunk = chunk_ref[2 * j, half, cut], chunk_ref[2 * j + 1, half, cut]
+            for powers, chunks, state, factor in zip(power_refs, chunk_refs, states, scaled):
+                eighth = powers[2 * SUB - 2, :, cut], powers[2 * SUB - 1, :, cut]
+                chunk = chunks[2 * j, :, cut], chunks[2 * j + 1, :, cut]
                 after.append(added_product(product(factor, chunk), eighth, state))
             return tuple(after)
 
@@ -423,22 +438,32 @@
     where, grad_out = lax.optimization_barrier((lax.axis_index(SEQ).reshape(1), grad_out))
     scalar = pl.BlockSpec(memory_space=pltpu.SMEM)
     whole = pl.BlockSpec(memory_space=pltpu.VMEM)
-    keep, send, weighted, chunks, powers, scale = pl.pallas_call(
-        local_kernel,
+    chunk_shape, power_shape = on_chip(2 * rows // SUB, SUB, width), on_chip(2 * SUB, SUB, width)
+    send, other_chunks, other_powers, weighted, stored, lags, base, scale = pl.pallas_call(
+        first_kernel,
         in_specs=[scalar] + [whole] * 6,
         out_shape=(
             on_chip(6, SUB, width),
-            on_chip(6, SUB, width),
+            chunk_shape,
+            power_shape,
             on_chip(rows, width),
-            on_chip(2 * rows // SUB, modes, width),
-            on_chip(2 * SUB, modes, width),
-            on_chip(modes, width),
+            on_chip(rows, width),
+            on_chip(SUB, SUB, width),
+            on_chip(2, SUB, width),
+            on_chip(SUB, width),
         ),
-        scratch_shapes=[pltpu.VMEM((rows, width), jnp.float32)],
-        name="local_pass",
+        name="first_half",
     )(where, grad_out, gate_query, key_input, value_input, decay_rate, pole_angle)
+    got = kept(lax.ppermute(send, SEQ, flip))
+    weighted = kept(weighted)
+    keep, chunks, powers = pl.pallas_call(
+        second_kernel,
+        in_specs=[whole] * 5,
+        out_shape=(on_chip(6, SUB, width), chunk_shape, power_shape),
+        cost_estimate=pl.CostEstimate(flops=20 * rows * width * modes, bytes_accessed=12 * rows * width, transcendentals=0),
+        name="second_half",
+    )(weighted, kept(stored), kept(lags), kept(base), kept(scale))
     keep, powers = kept(keep), kept(powers)
-    got = kept(lax.ppermute(send, SEQ, flip))
     packed = pl.pallas_call(
         functools.partial(chip_kernel, rows),
         in_specs=[scalar] + [whole] * 3,
@@ -475,14 +500,14 @@
     all_squares = kept(lax.all_to_all(squares, ("core", "chan"), 0, 0, tiled=True))
     grad_key, grad_value = pl.pallas_call(
         signal_kernel,
-        in_specs=[scalar] + [whole] * 10,
+        in_specs=[scalar] + [whole] * 12,
         out_shape=(jax.ShapeDtypeStruct((rows, width), jnp.bfloat16),) * 2,
         scratch_shapes=[pltpu.VMEM((width // LANES, rows * SUB, LANES), jnp.float32)],
         cost_estimate=pl.CostEstimate(flops=20 * rows * width * modes, bytes_accessed=12 * rows * width, transcendentals=0),
         name="signal_pass",
     )(
-        where, mine, other, kept(weighted), kept(chunks), powers, kept(scale), kept(key_input), kept(value_input),
-        kept(residue), skip_gain.reshape(1, width),
+        where, mine, other, weighted, kept(chunks), kept(other_chunks), powers, kept(other_powers), kept(decay_rate),
+        kept(key_input), kept(value_input), kept(residue), skip_gain.reshape(1, width),
     )
     clip_level = math.sqrt(2 * modes * width * chan_shards)
     grad_residue = pl.pallas_call(

time: 85.4 us -> 84.8 us (level)
  waiting for transfers between devices: 5.07 us -> 4.13 us
    ppermute x1, waiting for transfers between devices: 0.92 us -> 0.01 us  [on_device(): got = kept(lax.ppermute(send, SEQ, flip))]
    pallas_call x2 -> x3, Pallas kernels: 6.45 us -> 6.46 us  [the longest x1 2.73 us: on_device(): pl.pallas_call(signal_kernel, in_specs=[scalar] + [whole] * 12, out_shape...]
  transfers between devices with their start and end apart: 3 -> 3, of which waited for: 2 -> 1; matrix products, arithmetic and copies ran while one was open for 0% -> 0% of each run, Pallas kernels for 3% -> 5%
where the time goes in v6:
time: 84.8 us; the launch traced here: 84.4 us
  blocking collectives  42.4 us (50%)
  starting transfers between devices  28.8 us (34%)
  Pallas kernels  8.33 us (10%)
  waiting for transfers between devices  4.13 us (5%)
    all_to_all x3, blocking collectives, exchange(): lax.all_to_all(sent, SEQ, 0, 0, tiled=True, axis_index_groups=over)  42.4 us
    ppermute x1, starting transfers between devices, on_device(): got = kept(lax.ppermute(send, SEQ, flip))  16.1 us
    all_to_all x1, starting transfers between devices, on_device(): lax.all_to_all(squares, ('core', 'chan'), 0, 0, tiled=True)  7.24 us
    ppermute x1, starting transfers between devices, on_device(): other = kept(lax.ppermute(send, SEQ, flip))  5.45 us
    all_to_all x1, waiting for transfers between devices, on_device(): lax.all_to_all(squares, ('core', 'chan'), 0, 0, tiled=True)  4.12 us
    pallas_call x1, Pallas kernels, on_device(): pl.pallas_call(signal_kernel, in_specs=[scalar] + [whole] * 12, out_shape...  2.73 us
    pallas_call x1, Pallas kernels, on_device(): pl.pallas_call(first_kernel, in_specs=[scalar] + [whole] * 6, out_shape=(...  2.63 us
  transfers between devices with their start and end apart: 3, of which 1 were waited for; matrix products, arithmetic and copies ran while one was open for 0% of the time, Pallas kernels for 5%

profile of v6, /device:TPU:1, one launch (start us, length us, event | category | flops | bytes accessed | tf_op | source)
XLA Modules:
  0.0 84.4 jit_solution(410644073622858114)
XLA Ops:
  0.6 2.6 %first_half.1 = (f32[6,8,512]{2,1,0:T(8,128)S(1)}, f32[32,8,512]{2,1,0:T(8,128)S(1)}, f32[16,8,512]{2,1,0:T(8,128)S(1)}, f32[128,512]{1,0:T(8,128)S(1)}, f32[128...) custom-call(s32[1]{0:T(128)} %bitcast.where_ref, ...), custom_call_target="tpu_custom_call" | custom-call | tf_op jit(solution)/shard_map/first_half/pallas_call | solution.py:442
  3.3 16.1 %collective-permute-start = (f32[6,8,512]{2,1,0:T(8,128)S(1)}, f32[6,8,512]{2,1,0:T(8,128)S(1)}, u32[]{:S(2)}, u32[]{:S(2)}) collective-permute-start(f32[6,8,512]{2,1,0:T(8,128)S(1)} %get-tuple-element.32), channel_id=1, source_target_pairs={{0,8},{8,0},{16,24},{24,16},{32,40},{40,32},{48,56},{56,48},{64,72... | collective-permute-start | bytes 294920 | tf_op jit(solution)/shard_map/ppermute | solution.py:457
  19.3 1.1 %second_half.1 = (f32[6,8,512]{2,1,0:T(8,128)S(1)}, f32[32,8,512]{2,1,0:T(8,128)S(1)}, f32[16,8,512]{2,1,0:T(8,128)S(1)}) custom-call(f32[128,512]{1,0:T(8,128)S(1)} %get-tuple-element.26.weighted, f32[128,512]{1,0:T(8,128)S(1)} %get-tuple-element.27.stored, f32[8,8,512]{2,1,0:T(8,128)S(1)} %get-tuple-element.28.lag_ref, ...), custom_call_target="tpu_custom_call" | custom-call | flops 20971520 | bytes 786432 | tf_op jit(solution)/shard_map/second_half/pallas_call | solution.py:459
  20.4 0.0 collective-permute-done.got_ref
  20.5 0.1 join_chip.1
  20.6 0.0 copy-start.2
  20.6 0.0 copy-start.3
  20.6 17.7 %all_to_all.38 = f32[16,1,1536]{2,1,0:T(1,128)S(1)} all-to-all(f32[16,1,1536]{2,1,0:T(1,128)S(1)} %bitcast.13), channel_id=1, replica_groups={{0,16,32,48,64,80,96,112,128,144,160,176,192,208,224,240},{8,24,40,56,7..., dimensions={0} | all-to-all | bytes 196608 | tf_op jit(solution)/shard_map/all_to_all | solution.py:524
  38.3 0.0 copy-done.2
  38.3 0.0 copy-done.3
  38.3 0.2 join_run.1
  38.5 8.1 %all_to_all.39 = f32[4,1,1536]{2,1,0:T(1,128)S(1)} all-to-all(f32[4,1,1536]{2,1,0:T(1,128)S(1)} %bitcast.18), channel_id=1, replica_groups={{0,256,512,768},{8,264,520,776},{16,272,528,784},{24,280,536,792},{32,2..., dimensions={0} | all-to-all | bytes 49152 | tf_op jit(solution)/shard_map/all_to_all | solution.py:524
  46.6 0.1 join_runs.1
  46.7 16.6 %all_to_all.40 = f32[16,1,1024]{2,1,0:T(1,128)S(1)} all-to-all(f32[16,1,1024]{2,1,0:T(1,128)S(1)} %bitcast.15), channel_id=1, replica_groups={{0,16,32,48,64,80,96,112,128,144,160,176,192,208,224,240},{8,24,40,56,7..., dimensions={0} | all-to-all | bytes 131072 | tf_op jit(solution)/shard_map/all_to_all | solution.py:524
  63.3 0.7 residue_sums.1
  64.0 5.5 %collective-permute-start.1 = (f32[4,8,512]{2,1,0:T(8,128)S(1)}, f32[4,8,512]{2,1,0:T(8,128)S(1)}, u32[]{:S(2)}, u32[]{:S(2)}) collective-permute-start(f32[4,8,512]{2,1,0:T(8,128)S(1)} %get-tuple-element.38), channel_id=1, source_target_pairs={{0,8},{8,0},{16,24},{24,16},{32,40},{40,32},{48,56},{56,48},{64,72... | collective-permute-start | bytes 196616 | tf_op jit(solution)/shard_map/ppermute | solution.py:498
  69.5 7.2 %all-to-all-start.3 = ((f32[16,1,128]{2,1,0:T(1,128)}), f32[16,1,128]{2,1,0:T(1,128)S(1)}, u32[]{:S(2)}, u32[]{:S(2)}) async-start(f32[16,1,128]{2,1,0:T(1,128)} %bitcast.9), calls=%async_computation.3 | async-start | bytes 16384 | tf_op jit(solution)/shard_map/all_to_all | solution.py:500
  76.7 0.0 collective-permute-done.1.other_ref
  76.7 0.0 copy-done
  76.7 0.0 copy-done.1
  76.7 0.0 copy-done.4
  76.7 2.7 %signal_pass.1 = (bf16[128,512]{1,0:T(8,128)(2,1)}, bf16[128,512]{1,0:T(8,128)(2,1)}) custom-call(s32[1]{0:T(128)} %bitcast.where_ref, f32[4,8,512]{2,1,0:T(8,128)S(1)} %get-tuple-element.37.mine_ref, f32[4,8,512]{2,1,0:T(8,128)S(1)} %collective-permute-done.1.other_ref, f32[128,512]{1,0:T(8,128)S(1)} %get-tuple-element.26.weighted, ...), custom_call_target="tpu_custom_call" | custom-call | flops 20971520 | bytes 786432 | tf_op jit(solution)/shard_map/signal_pass/pallas_call | solution.py:501
  79.5 4.1 %all-to-all-done.3 = f32[16,1,128]{2,1,0:T(1,128)S(1)} async-done(((f32[16,1,128]{2,1,0:T(1,128)}), f32[16,1,128]{2,1,0:T(1,128)S(1)}, u32[]{:S(2)}, u32[]{:S(2)}) %all-to-all-start.3) | async-done | bytes 8224 | tf_op jit(solution)/shard_map/all_to_all | solution.py:500
  83.6 0.8 clip.1
  (3 shorter events, 0.0 us)
Async XLA Ops:
  3.3 17.2 %collective-permute-start = (f32[6,8,512]{2,1,0:T(8,128)S(1)}, f32[6,8,512]{2,1,0:T(8,128)S(1)}, u32[]{:S(2)}, u32[]{:S(2)}) collective-permute-start(f32[6,8,512]{2,1,0:T(8,128)S(1)} %get-tuple-element.32), channel_id=1, source_target_pairs={{0,8},{8,0},{16,24},{24,16},{32,40},{40,32},{48,56},{56,48},{64,72... | collective-permute-start | bytes 294920 | tf_op jit(solution)/shard_map/ppermute | solution.py:457
  20.6 17.7 %copy-start.2 = (f32[16,512]{1,0:T(8,128)S(1)}, f32[16,512]{1,0:T(8,128)}, u32[]{:S(2)}) copy-start(f32[16,512]{1,0:T(8,128)} %decay_ref.5) | copy-start | bytes 98308
  20.6 17.7 %copy-start.3 = (f32[16,512]{1,0:T(8,128)S(1)}, f32[16,512]{1,0:T(8,128)}, u32[]{:S(2)}) copy-start(f32[16,512]{1,0:T(8,128)} %angle_ref.3) | copy-start | bytes 98308
  63.3 13.4 %copy-start = (bf16[128,512]{1,0:T(8,128)(2,1)S(1)}, bf16[128,512]{1,0:T(8,128)(2,1)}, u32[]{:S(2)}) copy-start(bf16[128,512]{1,0:T(8,128)(2,1)} %key_ref.3) | copy-start | bytes 393220
  63.3 13.4 %copy-start.1 = (bf16[128,512]{1,0:T(8,128)(2,1)S(1)}, bf16[128,512]{1,0:T(8,128)(2,1)}, u32[]{:S(2)}) copy-start(bf16[128,512]{1,0:T(8,128)(2,1)} %value_ref.3) | copy-start | bytes 393220
  63.3 13.4 %copy-start.4 = (f32[2,16,512]{2,1,0:T(8,128)S(1)}, f32[2,16,512]{2,1,0:T(8,128)}, u32[]{:S(2)}) copy-start(f32[2,16,512]{2,1,0:T(8,128)} %residue_ref.1) | copy-start | bytes 196612
  64.0 12.7 %collective-permute-start.1 = (f32[4,8,512]{2,1,0:T(8,128)S(1)}, f32[4,8,512]{2,1,0:T(8,128)S(1)}, u32[]{:S(2)}, u32[]{:S(2)}) collective-permute-start(f32[4,8,512]{2,1,0:T(8,128)S(1)} %get-tuple-element.38), channel_id=1, source_target_pairs={{0,8},{8,0},{16,24},{24,16},{32,40},{40,32},{48,56},{56,48},{64,72... | collective-permute-start | bytes 196616 | tf_op jit(solution)/shard_map/ppermute | solution.py:498
  69.5 14.1 %all-to-all-start.3 = ((f32[16,1,128]{2,1,0:T(1,128)}), f32[16,1,128]{2,1,0:T(1,128)S(1)}, u32[]{:S(2)}, u32[]{:S(2)}) async-start(f32[16,1,128]{2,1,0:T(1,128)} %bitcast.9), calls=%async_computation.3 | async-start | bytes 16384 | tf_op jit(solution)/shard_map/all_to_all | solution.py:500
